TPU v7x, 128 devices: a whole 4x4x4 slice. The times are simulated.
128 devices in a mesh: dp: 4 (over z), rows: 32 (over x, y, core).
Axes of the slice: x: 4, y: 4, z: 4, core: 2. Of those that a mesh axis runs over, the one named last changes fastest.
Arguments:
- owners: int32 [131072, 1], P(('dp', 'rows')), may hold values from 0 to 127; in each aligned block of 1024 rows (0 to 1023, 1024 to 2047, ...) at most 32 rows name the same one
- offsets: int32 [131072], P(('dp', 'rows')), may hold values from 0 to 8191
- gradients: bfloat16 [131072, 128], P(('dp', 'rows')), may hold values from -6 to 6
- embedding: float32 [1048576, 128], P(('dp', 'rows')), may hold values from -6 to 6
- adagrad_state: float32 [1048576], P(('dp', 'rows')), may hold values from 0.05 to 2
- next_owners: int32 [131072, 1], P(('dp', 'rows')), may hold values from 0 to 127; in each aligned block of 1024 rows (0 to 1023, 1024 to 2047, ...) at most 32 rows name the same one
- next_offsets: int32 [131072], P(('dp', 'rows')), may hold values from 0 to 8191
Outputs:
- new_embedding: float32 [1048576, 128], P(('dp', 'rows'))
- new_state: float32 [1048576], P(('dp', 'rows'))
- next_rows: bfloat16 [131072, 128], P(('dp', 'rows'))
Inputs may be any that keep to these rules, and one draw needn't show every extreme that they name: `owners`: within the 1024 rows of one device, at most 32 rows name the same block. `next_owners`: within the 1024 rows of one device, at most 32 rows name the same block.
All inputs are finite; a program needn't handle non-finite values.
Results may differ from a plain program's by a relative error of at most 0.0013.
Values may be sent and summed in bfloat16 or wider, within the bound.
No kernel may reach another device: no remote copies, remote signals or barrier semaphores. Data moves between devices by JAX's collectives and lax.ppermute only.
A program may use at most 64 MiB of HBM per device.

v0:
```python
import jax
import jax.numpy as jnp
from jax import lax
from jax.sharding import PartitionSpec as P


def split_up(x, dim, count):
    before, after = (x.shape[:dim], x.shape[dim + 1 :])
    return jnp.moveaxis(x.reshape(*before, count, -1, *after), dim, 0)


def laid_out(parts, dim):
    lengths = list(parts.shape[1:])
    lengths[dim] *= parts.shape[0]
    return jnp.moveaxis(parts, 0, dim).reshape(lengths)


def exchange_both(x, axis, axes, splits, concats):
    sizes = [lax.axis_size(a) for a in axes]
    parts = split_up(x, splits[0], sizes[0])
    parts = jnp.moveaxis(split_up(parts, splits[1] + 1, sizes[1]), 0, 1)
    inside = parts.shape[2:]
    parts = parts.reshape(-1, *inside)
    parts = lax.all_to_all(parts, axis, split_axis=0, concat_axis=0, tiled=True)
    parts = laid_out(parts.reshape(*sizes, *inside), concats[0] + 1)
    return laid_out(parts, concats[1])


def assign_slots(owner_ids, active, devices):
    lookups = owner_ids.shape[0]
    one_hot = (
        (owner_ids[:, None] == jnp.arange(devices, dtype=jnp.int32)[None, :]) & active[:, None]
    ).astype(jnp.bfloat16)
    positions = jnp.arange(lookups, dtype=jnp.int32)
    earlier = (positions[:, None] > positions[None, :]).astype(jnp.bfloat16)
    ahead_count = jnp.dot(earlier, one_hot, preferred_element_type=jnp.float32)
    return jnp.take_along_axis(ahead_count, owner_ids[:, None], axis=1)[:, 0].astype(jnp.int32)


def on_device(owners, offsets, gradients, embedding, adagrad_state, next_owners, next_offsets):
    devices = lax.axis_size(("dp", "rows"))
    lookups = gradients.shape[0]
    columns = gradients.shape[1]
    owned_rows = embedding.shape[0]
    capacity = max(2, 4 * lookups // devices)
    owner_ids = owners[:, 0]
    active = jnp.ones((lookups,), bool)
    slot_ids = assign_slots(owner_ids, active, devices)
    target = jnp.where(active, owner_ids, devices)
    outgoing = (
        jnp.zeros((devices, capacity, columns), gradients.dtype)
        .at[target, slot_ids]
        .set(gradients, mode="drop")
    )
    slot_rows = (
        jnp.zeros((devices, capacity), jnp.int32).at[target, slot_ids].set(offsets, mode="drop")
    )
    dp_count = lax.axis_size("dp")
    row_count = lax.axis_size("rows")
    sectioned = outgoing.reshape(dp_count, row_count, capacity, columns)
    sectioned_rows = slot_rows.reshape(dp_count, row_count, capacity)
    incoming, incoming_rows = (
        exchange_both(sectioned, ("dp", "rows"), ("dp", "rows"), (0, 1), (0, 1)),
        exchange_both(sectioned_rows, ("dp", "rows"), ("dp", "rows"), (0, 1), (0, 1)),
    )
    incoming = incoming.reshape(-1, columns).astype(jnp.float32)
    incoming_rows = incoming_rows.reshape(-1)
    grad_sum = jnp.zeros((owned_rows, columns), jnp.float32).at[incoming_rows].add(incoming)
    new_state = adagrad_state + jnp.mean(grad_sum * grad_sum, axis=1)
    new_embedding = embedding - 0.5 * grad_sum / jnp.sqrt(new_state)[:, None]
    table_half = new_embedding.astype(jnp.bfloat16)
    wanted = next_owners[:, 0]
    next_slots = assign_slots(wanted, jnp.ones((lookups,), bool), devices)
    requests = jnp.zeros((devices, capacity), jnp.int32).at[wanted, next_slots].set(next_offsets)
    fetched = table_half[
        lax.all_to_all(requests, ("dp", "rows"), split_axis=0, concat_axis=0, tiled=True)
    ]
    returned = lax.all_to_all(fetched, ("dp", "rows"), split_axis=0, concat_axis=0, tiled=True)
    next_rows = returned[wanted, next_slots]
    return (new_embedding, new_state, next_rows)


def solution(mesh):
    in_specs = (
        P(("dp", "rows"), None),
        P(("dp", "rows")),
        P(("dp", "rows"), None),
        P(("dp", "rows"), None),
        P(("dp", "rows")),
        P(("dp", "rows"), None),
        P(("dp", "rows")),
    )
    out_specs = (P(("dp", "rows"), None), P(("dp", "rows")), P(("dp", "rows"), None))
    return jax.shard_map(
        on_device, mesh=mesh, in_specs=in_specs, out_specs=out_specs, check_vma=False
    )
```

profile of v0, /device:TPU:1, one launch (start us, length us, event | category | flops | bytes accessed | tf_op | source)
XLA Modules:
  0.0 169.4 jit_solution(4949305938149009518)
XLA Ops:
  0.7 0.7 compare_select_fusion.5
  1.4 0.7 fusion.24
  2.1 0.7 compare_select_fusion.3
  2.8 0.7 fusion.23
  3.5 1.5 fusion
  5.1 6.8 %gather_fusion.3 = f32[1024]{0:T(1024)S(1)} fusion(f32[1024,128]{1,0:T(8,128)S(1)} %fusion, s32[1024]{0:T(1024)S(1)} %bitcast.61), kind=kCustom, calls=%fused_computation.1.clone | custom fusion | bytes 16384 | tf_op jit(solution)/shard_map/jit(take_along_axis)/gather | solution.py:37
  11.9 0.0 copy-start.5
  11.9 0.0 copy-start.6
  12.0 0.8 fusion.1
  12.8 6.8 %gather_fusion.2 = f32[1024]{0:T(1024)S(1)} fusion(f32[1024,128]{1,0:T(8,128)S(1)} %fusion.1, s32[1024]{0:T(1024)S(1)} %bitcast.60), kind=kCustom, calls=%fused_computation.clone | custom fusion | bytes 16384 | tf_op jit(solution)/shard_map/jit(take_along_axis)/gather | solution.py:37
  19.6 0.1 and_reduce_fusion
  19.8 0.1 multiply_reduce_fusion.2
  19.9 4.5 %scatter_custom_fusion.1 = s32[4096]{0:T(1024)S(1)} fusion(s32[1024]{0:T(1024)S(1)} %get-tuple-element.18, s32[1024]{0:T(1024)} %param.10, s32[]{:T(128)} %constant.17.clone.1), kind=kCustom, calls=%fused_computation.42 | custom fusion | bytes 16896
  24.4 0.7 copy.12
  25.1 11.5 %all-to-all-start = ((s32[128,1,1,32]{3,2,1,0:T(1,128)}), s32[128,1,1,32]{3,2,1,0:T(1,128)S(1)}, u32[]{:S(2)}, u32[]{:S(2)}) async-start(s32[128,1,1,32]{3,2,1,0:T(1,128)} %copy.12), calls=%async_computation | async-start | bytes 131072 | tf_op jit(solution)/shard_map/all_to_all | solution.py:24
  36.6 4.5 %scatter_custom_fusion.3 = s32[4096]{0:T(1024)S(1)} fusion(s32[1024]{0:T(1024)S(1)} %broadcast_select_fusion, s32[1024]{0:T(1024)} %param.15, s32[]{:T(128)} %constant.17.clone.1), kind=kCustom, calls=%fused_computation.40 | custom fusion | bytes 16896
  41.1 0.7 copy.14
  41.8 4.3 %all-to-all-done = s32[128,1,1,32]{3,2,1,0:T(1,128)S(1)} async-done(((s32[128,1,1,32]{3,2,1,0:T(1,128)}), s32[128,1,1,32]{3,2,1,0:T(1,128)S(1)}, u32[]{:S(2)}, u32[]{:S(2)}) %all-to-all-start) | async-done | bytes 16416 | tf_op jit(solution)/shard_map/all_to_all | solution.py:24
  46.2 5.4 %all-to-all-start.2 = ((s32[128,1,32]{2,1,0:T(1,128)}), s32[128,1,32]{2,1,0:T(1,128)S(1)}, u32[]{:S(2)}, u32[]{:S(2)}) async-start(s32[128,1,32]{2,1,0:T(1,128)} %copy.14), calls=%async_computation.2 | async-start | bytes 131072 | tf_op jit(solution)/shard_map/all_to_all | solution.py:76
  51.6 4.6 %scatter_custom_fusion.2 = bf16[4096,128]{1,0:T(8,128)(2,1)} fusion(s32[1024]{0:T(1024)S(1)} %get-tuple-element.17, bf16[1024,128]{1,0:T(8,128)(2,1)} %param.11, bf16[]{:T(256)} %constant.2.clone.1), kind=kCustom, calls=%fused_computation.16 | custom fusion | bytes 1049088
  56.2 0.1 reshape_reshape.4
  56.3 4.9 %all-to-all-done.2 = s32[128,1,32]{2,1,0:T(1,128)S(1)} async-done(((s32[128,1,32]{2,1,0:T(1,128)}), s32[128,1,32]{2,1,0:T(1,128)S(1)}, u32[]{:S(2)}, u32[]{:S(2)}) %all-to-all-start.2) | async-done | bytes 16416 | tf_op jit(solution)/shard_map/all_to_all | solution.py:76
  61.2 4.9 %all-to-all-start.1 = ((bf16[128,1,1,32,128]{4,3,2,1,0:T(8,128)(2,1)}), bf16[128,1,1,32,128]{4,3,2,1,0:T(8,128)(2,1)S(1)}, u32[]{:S(2)}, u32[]{:S(2)}) async-start(bf16[128,1,1,32,128]{4,3,2,1,0:T(8,128)(2,1)} %bitcast.14), calls=%async_computation.1 | async-start | bytes 2097152 | tf_op jit(solution)/shard_map/all_to_all | solution.py:24
  66.1 0.1 reshape.132
  66.2 18.7 %all-to-all-done.1 = bf16[128,1,1,32,128]{4,3,2,1,0:T(8,128)(2,1)S(1)} async-done(((bf16[128,1,1,32,128]{4,3,2,1,0:T(8,128)(2,1)}), bf16[128,1,1,32,128]{4,3,2,1,0:T(8,128)(2,1)S(1)}, u32[]{:S(2)}, u32[]{:S(2)}) %all-to-all-start.1) | async-done | bytes 1048608 | tf_op jit(solution)/shard_map/all_to_all | solution.py:24
  84.9 28.6 %scatter_custom_fusion = f32[8192,128]{1,0:T(8,128)} fusion(s32[4096]{0:T(1024)S(1)} %bitcast.70, bf16[4096,128]{1,0:T(8,128)(2,1)S(1)} %bitcast.63, f32[]{:T(128)} %constant.16.clone.1), kind=kCustom, calls=%fused_computation.13 | custom fusion | flops 1048576 | bytes 5242884 | tf_op jit(solution)/shard_map/scatter-add | solution.py:68
  113.5 3.5 %multiply_reduce_fusion = f32[8192]{0:T(1024)S(1)} fusion(f32[8192,128]{1,0:T(8,128)} %scatter_custom_fusion), kind=kLoop, calls=%fused_computation.9 | loop fusion | flops 2088960 | bytes 4227072 | tf_op jit(solution)/shard_map/reduce_sum | solution.py:69
  117.0 0.6 fusion.22
  117.6 6.6 %fusion.21 = (bf16[8192,128]{1,0:T(8,128)(2,1)S(1)}, f32[8192,128]{1,0:T(8,128)}) fusion(f32[8192,128]{1,0:T(8,128)} %param.12, f32[8192]{0:T(1024)S(1)} %get-tuple-element.13, f32[8192,128]{1,0:T(8,128)S(1)} %copy-done), kind=kLoop, calls=%fused_computation.61 | loop fusion | flops 4194304 | bytes 14712832 | tf_op jit(solution)/shard_map/convert_element_type | solution.py:71
  124.2 12.1 %gather_fusion = bf16[4096,128]{1,0:T(8,128)(2,1)S(1)} fusion(bf16[8192,128]{1,0:T(8,128)(2,1)S(1)} %get-tuple-element.11, s32[4096]{0:T(1024)S(1)} %broadcast_clamp_fusion), kind=kCustom, calls=%fused_computation.2 | custom fusion | bytes 2113536 | tf_op jit(solution)/shard_map/gather | solution.py:75
  136.3 22.6 %all_to_all.27 = bf16[128,32,128]{2,1,0:T(8,128)(2,1)S(1)} all-to-all(bf16[128,32,128]{2,1,0:T(8,128)(2,1)S(1)} %bitcast.62), channel_id=1, replica_groups=mesh['dp'=4,'rows'=32] {'dp','rows'}, dimensions={0} | all-to-all | bytes 2097152 | tf_op jit(solution)/shard_map/all_to_all | solution.py:78
  158.9 10.5 %gather_fusion.1 = bf16[1024,128]{1,0:T(8,128)(2,1)} fusion(bf16[128,32,128]{2,1,0:T(8,128)(2,1)S(1)} %all_to_all.27, s32[1024]{0:T(1024)S(1)} %bitcast.59), kind=kCustom, calls=%fused_computation.3 | custom fusion | bytes 532480 | tf_op jit(solution)/shard_map/gather | solution.py:79
  (22 shorter events, 0.2 us)
Async XLA Ops:
  0.6 11.3 %copy-start.1 = (s32[1024,1]{0,1:T(1,128)S(1)}, s32[1024,1]{0,1:T(1,128)}, u32[]{:S(2)}) copy-start(s32[1024,1]{0,1:T(1,128)} %param.9) | copy-start | bytes 12292
  0.6 11.3 %copy-start.2 = (s32[1024,1]{0,1:T(1,128)S(1)}, s32[1024,1]{0,1:T(1,128)}, u32[]{:S(2)}) copy-start(s32[1024,1]{0,1:T(1,128)} %param.14) | copy-start | bytes 12292
  11.9 7.8 %copy-start.4 = (s32[2]{0:T(128)S(1)}, s32[2]{0:T(128)}, u32[]{:S(2)}) copy-start(s32[2]{0:T(128)} %constant.12) | copy-start | bytes 28
  11.9 7.9 %copy-start.5 = (s32[2]{0:T(128)S(1)}, s32[2]{0:T(128)}, u32[]{:S(2)}) copy-start(s32[2]{0:T(128)} %constant.15) | copy-start | bytes 28
  11.9 7.9 %copy-start.6 = (s32[2]{0:T(128)S(1)}, s32[2]{0:T(128)}, u32[]{:S(2)}) copy-start(s32[2]{0:T(128)} %constant.5) | copy-start | bytes 28
  25.1 21.1 %all-to-all-start = ((s32[128,1,1,32]{3,2,1,0:T(1,128)}), s32[128,1,1,32]{3,2,1,0:T(1,128)S(1)}, u32[]{:S(2)}, u32[]{:S(2)}) async-start(s32[128,1,1,32]{3,2,1,0:T(1,128)} %copy.12), calls=%async_computation | async-start | bytes 131072 | tf_op jit(solution)/shard_map/all_to_all | solution.py:24
  46.2 15.1 %all-to-all-start.2 = ((s32[128,1,32]{2,1,0:T(1,128)}), s32[128,1,32]{2,1,0:T(1,128)S(1)}, u32[]{:S(2)}, u32[]{:S(2)}) async-start(s32[128,1,32]{2,1,0:T(1,128)} %copy.14), calls=%async_computation.2 | async-start | bytes 131072 | tf_op jit(solution)/shard_map/all_to_all | solution.py:76
  61.2 23.7 %all-to-all-start.1 = ((bf16[128,1,1,32,128]{4,3,2,1,0:T(8,128)(2,1)}), bf16[128,1,1,32,128]{4,3,2,1,0:T(8,128)(2,1)S(1)}, u32[]{:S(2)}, u32[]{:S(2)}) async-start(bf16[128,1,1,32,128]{4,3,2,1,0:T(8,128)(2,1)} %bitcast.14), calls=%async_computation.1 | async-start | bytes 2097152 | tf_op jit(solution)/shard_map/all_to_all | solution.py:24
  84.9 32.1 %copy-start.3 = (f32[8192]{0:T(1024)S(1)}, f32[8192]{0:T(1024)}, u32[]{:S(2)}) copy-start(f32[8192]{0:T(1024)} %param.13) | copy-start | bytes 98308
  113.5 4.1 %copy-start = (f32[8192,128]{1,0:T(8,128)S(1)}, f32[8192,128]{1,0:T(8,128)}, u32[]{:S(2)}) copy-start(f32[8192,128]{1,0:T(8,128)} %scatter_custom_fusion) | copy-start | bytes 12582916
where the time goes:
time: 170 us; the launch traced here: 169 us
  local copies, waits for them, and re-layouts  51.5 us (30%)
  other arithmetic  42.5 us (25%)
  waiting for transfers between devices  27.9 us (16%)
  blocking collectives  22.6 us (13%)
  starting transfers between devices  21.8 us (13%)
  matrix products  2.32 us (1%)
    scatter-add x1, other arithmetic, on_device(): jnp.zeros((owned_rows, columns), jnp.float32).at[incoming_rows]  28.6 us
    all_to_all x2, waiting for transfers between devices, exchange_both(): parts = lax.all_to_all(parts, axis, split_axis=0, concat_axis=0, tiled=True)  23 us
    all_to_all x1, blocking collectives, on_device(): lax.all_to_all(fetched, ('dp', 'rows'), split_axis=0, concat_axis=0, tile...  22.6 us
    all_to_all x2, starting transfers between devices, exchange_both(): parts = lax.all_to_all(parts, axis, split_axis=0, concat_axis=0, tiled=True)  16.3 us
    unnamed x17, local copies, waits for them, and re-layouts  13.6 us
    gather x2, local copies, waits for them, and re-layouts, assign_slots(): jnp.take_along_axis(ahead_count, owner_ids[:, None], axis=1)[:, 0]  13.6 us
    gather x1, local copies, waits for them, and re-layouts, on_device(): table_half[lax.all_to_all(requests, ('dp', 'rows'), split_axis=0, concat_...  12.1 us
    gather x1, local copies, waits for them, and re-layouts, on_device(): next_rows = returned[wanted, next_slots]  10.5 us
  transfers between devices with their start and end apart: 3, of which 3 were waited for; matrix products, arithmetic and copies ran while one was open for 6% of the time, Pallas kernels for 0%

commit v1 on v0

v1 whole, which is shorter than its diff:
```python
import functools

import jax
import jax.numpy as jnp
from jax import lax
from jax.experimental import pallas as pl
from jax.experimental.pallas import tpu as pltpu
from jax.sharding import PartitionSpec as P

AXES = ("dp", "rows")
F32, BF16, I32 = jnp.float32, jnp.bfloat16, jnp.int32
LANES = 128
TABLES = 4


def iota(shape, dim):
    return lax.broadcasted_iota(I32, shape, dim)


def pack_kernel(cap, rows_out, own_ref, off_ref, nown_ref, noff_ref, g_ref, out_ref, q_ref,
                gf, outf, pos_v, pos_s, sem):
    blocks = own_ref.shape[0]
    devices = out_ref.shape[0]
    before = (iota((LANES, LANES), 0) < iota((LANES, LANES), 1)).astype(BF16)
    ones = jnp.ones((LANES, LANES), BF16)
    row = iota((LANES, LANES), 0)
    meta = jnp.zeros((devices, LANES), F32)

    def slots(o_ref, f_ref, first, meta):
        base = jnp.zeros((devices, LANES), F32)
        out = []
        for b in range(blocks):
            own = o_ref[b:b + 1, :]
            hit = iota((devices, LANES), 0) == own
            hot = hit.astype(BF16)
            ahead = jnp.dot(hot, before, preferred_element_type=F32) + base
            slot = jnp.sum(jnp.where(hit, ahead, 0.0), axis=0, keepdims=True).astype(I32)
            base = base + jnp.dot(hot, ones, preferred_element_type=F32)
            off = f_ref[b:b + 1, :]
            value = jnp.where(row < first + cap, off // LANES, off % LANES)
            here = (row >= first) & (row < first + 2 * cap) & (row % cap == slot)
            sel = jnp.where(here, value, 0).astype(F32).astype(BF16)
            meta = meta + lax.dot_general(hot, sel, (((1,), (1,)), ((), ())), preferred_element_type=F32)
            out.append((own, slot))
        return out, meta

    got, meta = slots(own_ref, off_ref, 0, meta)
    for b, (own, slot) in enumerate(got):
        pos_v[b:b + 1, :] = own * rows_out + slot
    copy = pltpu.make_async_copy(pos_v, pos_s, sem)
    copy.start()
    gf[...] = g_ref[...].astype(F32)
    outf[...] = jnp.zeros_like(outf)
    got, meta = slots(nown_ref, noff_ref, 2 * cap, meta)
    for b, (own, slot) in enumerate(got):
        q_ref[b:b + 1, :] = own * cap + slot
    outf[pl.ds(cap, devices, stride=rows_out), :] = meta
    copy.wait()

    for b in range(blocks):
        def step(i, carry, b=b):
            for k in range(16):
                j = i * 16 + k
                outf[pl.ds(pos_s[b, j], 1), :] = gf[pl.ds(b * LANES + j, 1), :]
            return carry
        lax.fori_loop(0, LANES // 16, step, 0)

    def narrow(d, carry):
        out_ref[d] = outf[pl.ds(pl.multiple_of(d * rows_out, 8), rows_out), :].astype(BF16)
        return carry
    lax.fori_loop(0, devices, narrow, 0, unroll=4)


def owner_kernel(cap, inc_ref, state_ref, emb_hbm, nemb_hbm, nstate_ref, ret_ref,
                 t0, t1, t2, t3, gf, metaf, idx_v, idx_s, emb, sems):
    devices, rows_in, columns = inc_ref.shape
    owned = emb.shape[0]
    tabs = (t0, t1, t2, t3)
    load = pltpu.make_async_copy(emb_hbm, emb, sems.at[0])
    load.start()

    def spread(d, carry):
        metaf[pl.ds(pl.multiple_of(d * 8, 8), 8), :] = inc_ref[d, cap:cap + 8, :].astype(F32)
        return carry
    lax.fori_loop(0, devices, spread, 0, unroll=8)
    m = metaf[pl.ds(0, devices, stride=8), :]
    idx_v[...] = (m * LANES + pltpu.roll(m, LANES - cap, 1)).astype(I32)
    copy = pltpu.make_async_copy(idx_v, idx_s, sems.at[1])
    copy.start()

    def widen(d, carry):
        gf[pl.ds(pl.multiple_of(d * cap, 8), cap), :] = inc_ref[d, 0:cap, :].astype(F32)
        return carry
    lax.fori_loop(0, devices, widen, 0, unroll=4)

    def clear(c, carry):
        for t in tabs:
            t[pl.ds(pl.multiple_of(c * 64, 64), 64), :] = jnp.zeros((64, columns), F32)
        return carry
    lax.fori_loop(0, owned // 64, clear, 0)
    copy.wait()

    def add(d, carry):
        for i in range(0, cap, TABLES):
            at = [pl.ds(idx_s[d, i + k], 1) for k in range(TABLES)]
            new = [tabs[k][at[k], :] + gf[pl.ds(d * cap + i + k, 1), :] for k in range(TABLES)]
            for k in range(TABLES):
                tabs[k][at[k], :] = new[k]
        return carry
    lax.fori_loop(0, devices, add, 0)
    load.wait()

    ones = jnp.ones((8, columns), BF16)
    per = 4
    nt = (((1,), (1,)), ((), ()))

    def update(c, carry):
        rows = pl.ds(pl.multiple_of(c * per * LANES, per * LANES), per * LANES)
        total = (t0[rows, :] + t1[rows, :]) + (t2[rows, :] + t3[rows, :])
        square = total * total
        high = square.astype(BF16)
        low = (square - high.astype(F32)).astype(BF16)
        mean = (lax.dot_general(ones, high, nt, preferred_element_type=F32)
                + lax.dot_general(ones, low, nt, preferred_element_type=F32)) * (1.0 / columns)
        for k in range(per):
            state = state_ref[pl.ds(c * per + k, 1), :] + mean[0:1, k * LANES:(k + 1) * LANES]
            nstate_ref[pl.ds(c * per + k, 1), :] = state
            scale = jnp.transpose(jnp.broadcast_to(0.5 / jnp.sqrt(state), (LANES, LANES)))
            here = pl.ds(pl.multiple_of((c * per + k) * LANES, LANES), LANES)
            emb[here, :] = emb[here, :] - total[k * LANES:(k + 1) * LANES, :] * scale
        pltpu.make_async_copy(emb.at[rows, :], nemb_hbm.at[rows, :], sems.at[2]).start()
        return carry
    lax.fori_loop(0, owned // (per * LANES), update, 0)

    def fetch(d, carry):
        for i in range(cap):
            gf[pl.ds(d * cap + i, 1), :] = emb[pl.ds(idx_s[d, 2 * cap + i], 1), :]
        return carry
    lax.fori_loop(0, devices, fetch, 0)

    def narrow(d, carry):
        ret_ref[d] = gf[pl.ds(pl.multiple_of(d * cap, 8), cap), :].astype(BF16)
        return carry
    lax.fori_loop(0, devices, narrow, 0, unroll=4)
    pltpu.make_async_copy(emb, nemb_hbm, sems.at[2]).wait()


def unpack_kernel(cap, q_ref, ret_ref, out_ref, wide, rows):
    devices = ret_ref.shape[0]

    def widen(d, carry):
        wide[pl.ds(pl.multiple_of(d * cap, 8), cap), :] = ret_ref[d].astype(F32)
        return carry
    lax.fori_loop(0, devices, widen, 0, unroll=4)
    for b in range(q_ref.shape[0]):
        def step(i, carry, b=b):
            for k in range(16):
                j = i * 16 + k
                rows[pl.ds(b * LANES + j, 1), :] = wide[pl.ds(q_ref[b, j], 1), :]
            return carry
        lax.fori_loop(0, LANES // 16, step, 0)
    out_ref[...] = rows[...].astype(BF16)


VM = pl.BlockSpec(memory_space=pltpu.VMEM)
SM = pl.BlockSpec(memory_space=pltpu.SMEM)
ANY = pl.BlockSpec(memory_space=pl.ANY)


def on_device(owners, offsets, gradients, embedding, adagrad_state, next_owners, next_offsets):
    devices = lax.axis_size(AXES)
    lookups, columns = gradients.shape
    owned = embedding.shape[0]
    cap = max(2, 4 * lookups // devices)
    rows_out = cap + 8
    blocks = lookups // LANES
    shape = jax.ShapeDtypeStruct
    view = lambda x: x.reshape(blocks, LANES)

    outgoing, q = pl.pallas_call(
        functools.partial(pack_kernel, cap, rows_out),
        out_shape=(shape((devices, rows_out, columns), BF16), shape((blocks, LANES), I32)),
        in_specs=[VM] * 5,
        out_specs=(VM, VM),
        scratch_shapes=[
            pltpu.VMEM((lookups, columns), F32),
            pltpu.VMEM((devices * rows_out, columns), F32),
            pltpu.VMEM((blocks, LANES), I32),
            pltpu.SMEM((blocks, LANES), I32),
            pltpu.SemaphoreType.DMA,
        ],
        name="pack",
    )(view(owners), view(offsets), view(next_owners), view(next_offsets), gradients)

    incoming = lax.all_to_all(outgoing, AXES, split_axis=0, concat_axis=0, tiled=True)

    new_embedding, new_state, fetched = pl.pallas_call(
        functools.partial(owner_kernel, cap),
        out_shape=(
            shape(embedding.shape, F32),
            shape((owned // LANES, LANES), F32),
            shape((devices, cap, columns), BF16),
        ),
        in_specs=[VM, VM, ANY],
        out_specs=(ANY, VM, VM),
        scratch_shapes=[pltpu.VMEM((owned, columns), F32)] * TABLES
        + [
            pltpu.VMEM((devices * cap, columns), F32),
            pltpu.VMEM((devices * 8, columns), F32),
            pltpu.VMEM((devices, LANES), I32),
            pltpu.SMEM((devices, LANES), I32),
            pltpu.VMEM((owned, columns), F32),
            pltpu.SemaphoreType.DMA((3,)),
        ],
        name="owner",
    )(incoming, adagrad_state.reshape(owned // LANES, LANES), embedding)

    returned = lax.all_to_all(fetched, AXES, split_axis=0, concat_axis=0, tiled=True)

    next_rows = pl.pallas_call(
        functools.partial(unpack_kernel, cap),
        out_shape=shape((lookups, columns), BF16),
        in_specs=[SM, VM],
        out_specs=VM,
        scratch_shapes=[
            pltpu.VMEM((devices * cap, columns), F32),
            pltpu.VMEM((lookups, columns), F32),
        ],
        name="unpack",
    )(q, returned)
    return (new_embedding, new_state.reshape(owned), next_rows)


def solution(mesh):
    line, block = P(AXES), P(AXES, None)
    return jax.shard_map(
        on_device,
        mesh=mesh,
        in_specs=(block, line, block, block, line, block, line),
        out_specs=(block, line, block),
        check_vma=False,
    )
```

time: 170 us -> 91.2 us (0.54)
  local copies, waits for them, and re-layouts: 51.5 us -> 0 us
  other arithmetic: 42.5 us -> 0 us
  blocking collectives: 22.6 us -> 57.5 us
  Pallas kernels: 0 us -> 32.5 us
  waiting for transfers between devices: 27.9 us -> 0 us
  starting transfers between devices: 21.8 us -> 0 us
  matrix products: 2.32 us -> 0 us
    gather x4 -> x0, local copies, waits for them, and re-layouts: 36.2 us -> none  [the longest x2 13.6 us: assign_slots(): jnp.take_along_axis(ahead_count, owner_ids[:, None], axis=1)[:, 0]]
    all_to_all x1 -> x2, blocking collectives: 22.6 us -> 57.5 us  [the longest x1 33.2 us: on_device(): lax.all_to_all(outgoing, AXES, split_axis=0, concat_axis=0, tiled=True)]
    pallas_call x0 -> x3, Pallas kernels: none -> 32.5 us  [the longest x1 21.9 us: on_device(): pl.pallas_call(functools.partial(owner_kernel, cap), out_shape=(shape(emb...]
    scatter-add x1 -> x0, other arithmetic: 28.6 us -> none  [on_device(): jnp.zeros((owned_rows, columns), jnp.float32).at[incoming_rows]]
    all_to_all x3 -> x0, waiting for transfers between devices: 27.9 us -> none  [the longest x2 23 us: exchange_both(): parts = lax.all_to_all(parts, axis, split_axis=0, concat_axis=0, tiled=True)]
    all_to_all x3 -> x0, starting transfers between devices: 21.8 us -> none  [the longest x2 16.3 us: exchange_both(): parts = lax.all_to_all(parts, axis, split_axis=0, concat_axis=0, tiled=True)]
    unnamed x17 -> x0, local copies, waits for them, and re-layouts: 13.6 us -> none
    convert_element_type x1 -> x0, other arithmetic: 6.6 us -> none  [on_device(): table_half = new_embedding.astype(jnp.bfloat16)]
  transfers between devices with their start and end apart: 3 -> 0, of which waited for: 3 -> 0; matrix products, arithmetic and copies ran while one was open for 6% -> 0% of each run, Pallas kernels for 0% -> 0%
where the time goes in v1:
time: 91.2 us; the launch traced here: 90.7 us
  blocking collectives  57.5 us (63%)
  Pallas kernels  32.5 us (36%)
    all_to_all x1, blocking collectives, on_device(): lax.all_to_all(outgoing, AXES, split_axis=0, concat_axis=0, tiled=True)  33.2 us
    all_to_all x1, blocking collectives, on_device(): lax.all_to_all(fetched, AXES, split_axis=0, concat_axis=0, tiled=True)  24.3 us
    pallas_call x1, Pallas kernels, on_device(): pl.pallas_call(functools.partial(owner_kernel, cap), out_shape=(shape(emb...  21.9 us
    pallas_call x1, Pallas kernels, on_device(): pl.pallas_call(functools.partial(pack_kernel, cap, rows_out), out_shape=(...  6.1 us
    pallas_call x1, Pallas kernels, on_device(): pl.pallas_call(functools.partial(unpack_kernel, cap), out_shape=shape((lo...  4.52 us

profile of v1, /device:TPU:1, one launch (start us, length us, event | category | flops | bytes accessed | tf_op | source)
XLA Modules:
  0.0 90.7 jit_solution(365082345102641104)
XLA Ops:
  0.6 6.1 %pack.1 = (bf16[128,40,128]{2,1,0:T(8,128)(2,1)}, s32[8,128]{1,0:T(8,128)}) custom-call(s32[8,128]{1,0:T(8,128)} %bitcast.7, s32[8,128]{1,0:T(8,128)} %bitcast.8, s32[8,128]{1,0:T(8,128)} %bitcast.9, s32[8,128]{1,0:T(8,128)} %bitcast.10, bf16[1024,128]{1,0:T(8,128)(2,1)} %g_ref.1), custom_call_target="tpu_custom_call" | custom-call | tf_op jit(solution)/shard_map/pack/pallas_call | solution.py:180
  6.7 33.2 %all_to_all.10.inc_ref = bf16[128,40,128]{2,1,0:T(8,128)(2,1)} all-to-all(bf16[128,40,128]{2,1,0:T(8,128)(2,1)} %get-tuple-element.8), channel_id=1, replica_groups=mesh['dp'=4,'rows'=32] {'dp','rows'}, dimensions={0} | all-to-all | bytes 2621440 | tf_op jit(solution)/shard_map/all_to_all | solution.py:195
  39.9 21.9 %owner.1 = (f32[8192,128]{1,0:T(8,128)}, f32[64,128]{1,0:T(8,128)}, bf16[128,32,128]{2,1,0:T(8,128)(2,1)}) custom-call(bf16[128,40,128]{2,1,0:T(8,128)(2,1)} %all_to_all.10.inc_ref, f32[64,128]{1,0:T(8,128)} %bitcast.6, f32[8192,128]{1,0:T(8,128)} %emb_hbm.1), custom_call_target="tpu_custom_call" | custom-call | tf_op jit(solution)/shard_map/owner/pallas_call | solution.py:197
  61.8 24.3 %all_to_all.11.ret_ref = bf16[128,32,128]{2,1,0:T(8,128)(2,1)} all-to-all(bf16[128,32,128]{2,1,0:T(8,128)(2,1)} %get-tuple-element.12), channel_id=1, replica_groups=mesh['dp'=4,'rows'=32] {'dp','rows'}, dimensions={0} | all-to-all | bytes 2097152 | tf_op jit(solution)/shard_map/all_to_all | solution.py:218
  86.2 4.5 %unpack.1 = bf16[1024,128]{1,0:T(8,128)(2,1)} custom-call(s32[8,128]{1,0:T(8,128)} %get-tuple-element.11.q_ref, bf16[128,32,128]{2,1,0:T(8,128)(2,1)} %all_to_all.11.ret_ref), custom_call_target="tpu_custom_call" | custom-call | tf_op jit(solution)/shard_map/unpack/pallas_call | solution.py:220

commit v2 on v1

v2 whole, which is shorter than its diff:
```python
import functools

import jax
import jax.numpy as jnp
from jax import lax
from jax.experimental import pallas as pl
from jax.experimental.pallas import tpu as pltpu
from jax.sharding import PartitionSpec as P

AXES = ("dp", "rows")
F32, BF16, I32 = jnp.float32, jnp.bfloat16, jnp.int32
LANES = 128
TABLES = 4


def iota(shape, dim):
    return lax.broadcasted_iota(I32, shape, dim)


def pack_kernel(cap, rows_out, own_hbm, off_hbm, nown_hbm, noff_hbm, g_hbm, out_ref, q_ref,
                own_ref, off_ref, nown_ref, noff_ref, g_ref, gf, outf, pos_v, pos_s, sems):
    loads = [
        pltpu.make_async_copy(src, dst, sems.at[k])
        for k, (src, dst) in enumerate((
            (own_hbm, own_ref), (off_hbm, off_ref), (nown_hbm, nown_ref), (noff_hbm, noff_ref), (g_hbm, g_ref)
        ))
    ]
    for load in loads:
        load.start()
    outf[...] = jnp.zeros_like(outf)
    blocks = own_ref.shape[0]
    devices = out_ref.shape[0] // rows_out
    before = (iota((LANES, LANES), 0) < iota((LANES, LANES), 1)).astype(BF16)
    ones = jnp.ones((LANES, LANES), BF16)
    row = iota((LANES, LANES), 0)
    meta = jnp.zeros((devices, LANES), F32)

    def slots(o_ref, f_ref, first, meta):
        base = jnp.zeros((devices, LANES), F32)
        out = []
        for b in range(blocks):
            own = o_ref[b:b + 1, :]
            hit = iota((devices, LANES), 0) == own
            hot = hit.astype(BF16)
            ahead = jnp.dot(hot, before, preferred_element_type=F32) + base
            slot = jnp.sum(jnp.where(hit, ahead, 0.0), axis=0, keepdims=True).astype(I32)
            base = base + jnp.dot(hot, ones, preferred_element_type=F32)
            off = f_ref[b:b + 1, :]
            value = jnp.where(row < first + cap, off // LANES, off % LANES)
            here = (row >= first) & (row < first + 2 * cap) & (row % cap == slot)
            sel = jnp.where(here, value, 0).astype(F32).astype(BF16)
            meta = meta + lax.dot_general(hot, sel, (((1,), (1,)), ((), ())), preferred_element_type=F32)
            out.append((own, slot))
        return out, meta

    loads[0].wait()
    loads[1].wait()
    got, meta = slots(own_ref, off_ref, 0, meta)
    for b, (own, slot) in enumerate(got):
        pos_v[b:b + 1, :] = own * rows_out + slot
    copy = pltpu.make_async_copy(pos_v, pos_s, sems.at[5])
    copy.start()
    for load in loads[2:]:
        load.wait()
    gf[...] = g_ref[...].astype(F32)
    got, meta = slots(nown_ref, noff_ref, 2 * cap, meta)
    for b, (own, slot) in enumerate(got):
        q_ref[b:b + 1, :] = own * cap + slot
    outf[pl.ds(cap, devices, stride=rows_out), :] = meta
    copy.wait()

    def place(b, carry):
        for j in range(LANES):
            outf[pl.ds(pos_s[b, j], 1), :] = gf[pl.ds(b * LANES + j, 1), :]
        return carry
    lax.fori_loop(0, blocks, place, 0)
    out_ref[...] = outf[...].astype(BF16)


def owner_kernel(cap, rows_in, inc_ref, state_hbm, emb_hbm, nemb_hbm, nstate_ref, ret_ref,
                 t0, t1, t2, t3, gf, idx_v, idx_s, emb, state_ref, sems):
    devices = idx_v.shape[0]
    owned, columns = emb.shape
    tabs = (t0, t1, t2, t3)
    gf[...] = inc_ref[...].astype(F32)
    m = gf[pl.ds(cap, devices, stride=rows_in), :]
    idx_v[...] = (m * LANES + pltpu.roll(m, LANES - cap, 1)).astype(I32)
    copy = pltpu.make_async_copy(idx_v, idx_s, sems.at[1])
    copy.start()

    def clear(c, carry):
        for t in tabs:
            t[pl.ds(pl.multiple_of(c * 64, 64), 64), :] = jnp.zeros((64, columns), F32)
        return carry
    lax.fori_loop(0, owned // 64, clear, 0)
    copy.wait()
    load = pltpu.make_async_copy(emb_hbm, emb, sems.at[0])
    load.start()
    load_state = pltpu.make_async_copy(state_hbm, state_ref, sems.at[3])
    load_state.start()

    def add(d, carry):
        for i in range(0, cap, TABLES):
            at = [pl.ds(idx_s[d, i + k], 1) for k in range(TABLES)]
            new = [tabs[k][at[k], :] + gf[pl.ds(d * rows_in + i + k, 1), :] for k in range(TABLES)]
            for k in range(TABLES):
                tabs[k][at[k], :] = new[k]
        return carry
    lax.fori_loop(0, devices, add, 0)
    load.wait()
    load_state.wait()

    ones = jnp.ones((8, columns), BF16)
    per = 4
    nt = (((1,), (1,)), ((), ()))

    def update(c, carry):
        rows = pl.ds(pl.multiple_of(c * per * LANES, per * LANES), per * LANES)
        total = (t0[rows, :] + t1[rows, :]) + (t2[rows, :] + t3[rows, :])
        square = total * total
        high = square.astype(BF16)
        low = (square - high.astype(F32)).astype(BF16)
        mean = (lax.dot_general(ones, high, nt, preferred_element_type=F32)
                + lax.dot_general(ones, low, nt, preferred_element_type=F32)) * (1.0 / columns)
        for k in range(per):
            state = state_ref[pl.ds(c * per + k, 1), :] + mean[0:1, k * LANES:(k + 1) * LANES]
            nstate_ref[pl.ds(c * per + k, 1), :] = state
            scale = jnp.transpose(jnp.broadcast_to(0.5 / jnp.sqrt(state), (LANES, LANES)))
            here = pl.ds(pl.multiple_of((c * per + k) * LANES, LANES), LANES)
            emb[here, :] = emb[here, :] - total[k * LANES:(k + 1) * LANES, :] * scale
        pltpu.make_async_copy(emb.at[rows, :], nemb_hbm.at[rows, :], sems.at[2]).start()
        return carry
    lax.fori_loop(0, owned // (per * LANES), update, 0)

    def fetch(d, carry):
        for i in range(cap):
            gf[pl.ds(d * cap + i, 1), :] = emb[pl.ds(idx_s[d, 2 * cap + i], 1), :]
        return carry
    lax.fori_loop(0, devices, fetch, 0)

    ret_ref[...] = gf[0:devices * cap, :].astype(BF16)
    pltpu.make_async_copy(emb, nemb_hbm, sems.at[2]).wait()


def unpack_kernel(q_any, ret_ref, out_ref, wide, rows, q_ref, sem):
    copy = pltpu.make_async_copy(q_any, q_ref, sem)
    copy.start()
    wide[...] = ret_ref[...].astype(F32)
    copy.wait()

    def take(b, carry):
        for j in range(LANES):
            rows[pl.ds(b * LANES + j, 1), :] = wide[pl.ds(q_ref[b, j], 1), :]
        return carry
    lax.fori_loop(0, q_ref.shape[0], take, 0)
    out_ref[...] = rows[...].astype(BF16)


VM = pl.BlockSpec(memory_space=pltpu.VMEM)
ANY = pl.BlockSpec(memory_space=pl.ANY)


def on_device(owners, offsets, gradients, embedding, adagrad_state, next_owners, next_offsets):
    devices = lax.axis_size(AXES)
    lookups, columns = gradients.shape
    owned = embedding.shape[0]
    cap = max(2, 4 * lookups // devices)
    rows_out = cap + 2
    blocks = lookups // LANES
    shape = jax.ShapeDtypeStruct
    view = lambda x: x.reshape(blocks, LANES)
    in_hbm = lambda x: pltpu.with_memory_space_constraint(x, pltpu.HBM)

    outgoing, q = pl.pallas_call(
        functools.partial(pack_kernel, cap, rows_out),
        out_shape=(shape((devices * rows_out, columns), BF16), shape((blocks, LANES), I32)),
        in_specs=[ANY] * 5,
        out_specs=(VM, VM),
        scratch_shapes=[pltpu.VMEM((blocks, LANES), I32)] * 4
        + [
            pltpu.VMEM((lookups, columns), BF16),
            pltpu.VMEM((lookups, columns), F32),
            pltpu.VMEM((devices * rows_out, columns), F32),
            pltpu.VMEM((blocks, LANES), I32),
            pltpu.SMEM((blocks, LANES), I32),
            pltpu.SemaphoreType.DMA((6,)),
        ],
        compiler_params=pltpu.CompilerParams(vmem_limit_bytes=12 << 20),
        name="pack",
    )(*map(in_hbm, (view(owners), view(offsets), view(next_owners), view(next_offsets), gradients)))

    def exchange(x, pairs):
        x = x.reshape(devices, pairs, 2, columns)
        x = lax.all_to_all(x, AXES, split_axis=0, concat_axis=0, tiled=True)
        return x.reshape(devices * pairs * 2, columns)

    incoming = exchange(outgoing, rows_out // 2)

    new_embedding, new_state, fetched = pl.pallas_call(
        functools.partial(owner_kernel, cap, rows_out),
        out_shape=(
            shape(embedding.shape, F32),
            shape((owned // LANES, LANES), F32),
            shape((devices * cap, columns), BF16),
        ),
        in_specs=[VM, ANY, ANY],
        out_specs=(ANY, VM, VM),
        scratch_shapes=[pltpu.VMEM((owned, columns), F32)] * TABLES
        + [
            pltpu.VMEM((devices * rows_out, columns), F32),
            pltpu.VMEM((devices, LANES), I32),
            pltpu.SMEM((devices, LANES), I32),
            pltpu.VMEM((owned, columns), F32),
            pltpu.VMEM((owned // LANES, LANES), F32),
            pltpu.SemaphoreType.DMA((4,)),
        ],
        compiler_params=pltpu.CompilerParams(vmem_limit_bytes=36 << 20),
        name="owner",
    )(incoming, in_hbm(adagrad_state.reshape(owned // LANES, LANES)), in_hbm(embedding))

    returned = lax.all_to_all(
        fetched.reshape(devices, cap, columns), AXES, split_axis=0, concat_axis=0, tiled=True
    ).reshape(devices * cap, columns)

    next_rows = pl.pallas_call(
        unpack_kernel,
        out_shape=shape((lookups, columns), BF16),
        in_specs=[ANY, VM],
        out_specs=VM,
        scratch_shapes=[
            pltpu.VMEM((devices * cap, columns), F32),
            pltpu.VMEM((lookups, columns), F32),
            pltpu.SMEM((blocks, LANES), I32),
            pltpu.SemaphoreType.DMA,
        ],
        compiler_params=pltpu.CompilerParams(vmem_limit_bytes=12 << 20),
        name="unpack",
    )(q, returned)
    return (new_embedding, new_state.reshape(owned), next_rows)


def solution(mesh):
    line, block = P(AXES), P(AXES, None)
    return jax.shard_map(
        on_device,
        mesh=mesh,
        in_specs=(block, line, block, block, line, block, line),
        out_specs=(block, line, block),
        check_vma=False,
    )
```

time: 91.2 us -> 80.5 us (0.88)
  Pallas kernels: 32.5 us -> 25.2 us
  blocking collectives: 57.5 us -> 54.5 us
    pallas_call x2, Pallas kernels: 26.4 us -> 22 us  [the longest x1 19.8 us: on_device(): pl.pallas_call(functools.partial(owner_kernel, cap, rows_out), out_shape=...]
    all_to_all x2, blocking collectives: 57.5 us -> 54.5 us  [the longest x1 30.8 us: exchange(): x = lax.all_to_all(x, AXES, split_axis=0, concat_axis=0, tiled=True)]
    pallas_call x1, Pallas kernels: 6.1 us -> 3.21 us  [on_device(): pl.pallas_call(functools.partial(pack_kernel, cap, rows_out), out_shape=(...]
where the time goes in v2:
time: 80.5 us; the launch traced here: 80.4 us
  blocking collectives  54.5 us (68%)
  Pallas kernels  25.2 us (31%)
    all_to_all x1, blocking collectives, exchange(): x = lax.all_to_all(x, AXES, split_axis=0, concat_axis=0, tiled=True)  30.8 us
    all_to_all x1, blocking collectives, on_device(): lax.all_to_all(fetched.reshape(devices, cap, columns), AXES, split_axis=0...  23.8 us
    pallas_call x1, Pallas kernels, on_device(): pl.pallas_call(functools.partial(owner_kernel, cap, rows_out), out_shape=...  19.8 us
    pallas_call x1, Pallas kernels, on_device(): pl.pallas_call(functools.partial(pack_kernel, cap, rows_out), out_shape=(...  3.21 us
    pallas_call x1, Pallas kernels, on_device(): pl.pallas_call(unpack_kernel, out_shape=shape((lookups, columns), BF16),...  2.18 us

profile of v2, /device:TPU:1, one launch (start us, length us, event | category | flops | bytes accessed | tf_op | source)
XLA Modules:
  0.0 80.4 jit_solution(763129146815544290)
XLA Ops:
  0.6 3.2 %pack.1 = (bf16[4352,128]{1,0:T(8,128)(2,1)S(1)}, s32[8,128]{1,0:T(8,128)S(1)}) custom-call(s32[8,128]{1,0:T(8,128)} %bitcast.15, s32[8,128]{1,0:T(8,128)} %bitcast.16, s32[8,128]{1,0:T(8,128)} %bitcast.17, s32[8,128]{1,0:T(8,128)} %bitcast.18, bf16[1024,128]{1,0:T(8,128)(2,1)} %g_hbm.1), custom_call_target="tpu_custom_call" | custom-call | tf_op jit(solution)/shard_map/pack/pallas_call | solution.py:174
  3.9 30.8 %all_to_all.10 = bf16[128,17,2,128]{3,2,1,0:T(2,128)(2,1)S(1)} all-to-all(bf16[128,17,2,128]{3,2,1,0:T(2,128)(2,1)S(1)} %bitcast.12), channel_id=1, replica_groups=mesh['dp'=4,'rows'=32] {'dp','rows'}, dimensions={0} | all-to-all | bytes 2228224 | tf_op jit(solution)/shard_map/all_to_all | solution.py:194
  34.6 19.8 %owner.1 = (f32[8192,128]{1,0:T(8,128)}, f32[64,128]{1,0:T(8,128)}, bf16[4096,128]{1,0:T(8,128)(2,1)S(1)}) custom-call(bf16[4352,128]{1,0:T(8,128)(2,1)S(1)} %bitcast.10, f32[64,128]{1,0:T(8,128)} %bitcast.14, f32[8192,128]{1,0:T(8,128)} %emb_hbm.1), custom_call_target="tpu_custom_call" | custom-call | tf_op jit(solution)/shard_map/owner/pallas_call | solution.py:199
  54.5 23.8 %all_to_all.11 = bf16[128,32,128]{2,1,0:T(8,128)(2,1)S(1)} all-to-all(bf16[128,32,128]{2,1,0:T(8,128)(2,1)S(1)} %bitcast.13), channel_id=1, replica_groups=mesh['dp'=4,'rows'=32] {'dp','rows'}, dimensions={0} | all-to-all | bytes 2097152 | tf_op jit(solution)/shard_map/all_to_all | solution.py:221
  78.2 2.2 %unpack.1 = bf16[1024,128]{1,0:T(8,128)(2,1)} custom-call(s32[8,128]{1,0:T(8,128)S(1)} %get-tuple-element.11.q_any, bf16[4096,128]{1,0:T(8,128)(2,1)S(1)} %bitcast.11), custom_call_target="tpu_custom_call" | custom-call | tf_op jit(solution)/shard_map/unpack/pallas_call | solution.py:225

commit v3 on v2

--- a/solution.py
+++ b/solution.py
@@ -46,7 +46,7 @@
             slot = jnp.sum(jnp.where(hit, ahead, 0.0), axis=0, keepdims=True).astype(I32)
             base = base + jnp.dot(hot, ones, preferred_element_type=F32)
             off = f_ref[b:b + 1, :]
-            value = jnp.where(row < first + cap, off // LANES, off % LANES)
+            value = jnp.where(row < first + cap, off // LANES + 1, off % LANES)
             here = (row >= first) & (row < first + 2 * cap) & (row % cap == slot)
             sel = jnp.where(here, value, 0).astype(F32).astype(BF16)
             meta = meta + lax.dot_general(hot, sel, (((1,), (1,)), ((), ())), preferred_element_type=F32)
@@ -56,89 +56,116 @@
     loads[0].wait()
     loads[1].wait()
     got, meta = slots(own_ref, off_ref, 0, meta)
-    for b, (own, slot) in enumerate(got):
-        pos_v[b:b + 1, :] = own * rows_out + slot
+    pos_v[:, 0:blocks] = jnp.transpose(jnp.concatenate([own * rows_out + slot for own, slot in got], axis=0))
     copy = pltpu.make_async_copy(pos_v, pos_s, sems.at[5])
     copy.start()
     for load in loads[2:]:
         load.wait()
     gf[...] = g_ref[...].astype(F32)
     got, meta = slots(nown_ref, noff_ref, 2 * cap, meta)
-    for b, (own, slot) in enumerate(got):
-        q_ref[b:b + 1, :] = own * cap + slot
+    q_ref[:, 0:blocks] = jnp.transpose(jnp.concatenate([own * cap + slot for own, slot in got], axis=0))
     outf[pl.ds(cap, devices, stride=rows_out), :] = meta
     copy.wait()
 
     def place(b, carry):
+        rows = gf.at[pl.ds(pl.multiple_of(b * LANES, LANES), LANES), :]
         for j in range(LANES):
-            outf[pl.ds(pos_s[b, j], 1), :] = gf[pl.ds(b * LANES + j, 1), :]
+            outf[pl.ds(pos_s.at[j][b], 1), :] = rows[j:j + 1, :]
         return carry
     lax.fori_loop(0, blocks, place, 0)
     out_ref[...] = outf[...].astype(BF16)
 
 
-def owner_kernel(cap, rows_in, inc_ref, state_hbm, emb_hbm, nemb_hbm, nstate_ref, ret_ref,
-                 t0, t1, t2, t3, gf, idx_v, idx_s, emb, state_ref, sems):
-    devices = idx_v.shape[0]
+def pick(x, lane):
+    return jnp.take_along_axis(x, jnp.full(x.shape, lane, I32), axis=1)
+
+
+def owner_kernel(cap, rows_in, inc_ref, state_hbm, emb_hbm, nemb_hbm, nstate_hbm, ret_ref,
+                 t0, t1, t2, t3, gf, idx_v, cols_v, emb, state_ref, nstate, scales, sems, idx_all):
+    devices = idx_v.shape[1]
     owned, columns = emb.shape
     tabs = (t0, t1, t2, t3)
     gf[...] = inc_ref[...].astype(F32)
     m = gf[pl.ds(cap, devices, stride=rows_in), :]
-    idx_v[...] = (m * LANES + pltpu.roll(m, LANES - cap, 1)).astype(I32)
-    copy = pltpu.make_async_copy(idx_v, idx_s, sems.at[1])
+    index = ((m - 1.0) * LANES + pltpu.roll(m, LANES - cap, 1)).astype(I32)
+    apart = iota((devices, LANES), 0) * cap + iota((devices, LANES), 1) % cap
+    idx_v[...] = jnp.transpose(jnp.where(index < 0, apart % owned, index))
+    slots = list(range(cap)) + list(range(2 * cap, 3 * cap))
+    copy = pltpu.make_async_copy(idx_v, idx_all, sems.at[1])
     copy.start()
-
-    def clear(c, carry):
-        for t in tabs:
-            t[pl.ds(pl.multiple_of(c * 64, 64), 64), :] = jnp.zeros((64, columns), F32)
-        return carry
-    lax.fori_loop(0, owned // 64, clear, 0)
-    copy.wait()
+    idx_s = [idx_all.at[i] for i in slots]
     load = pltpu.make_async_copy(emb_hbm, emb, sems.at[0])
     load.start()
     load_state = pltpu.make_async_copy(state_hbm, state_ref, sems.at[3])
     load_state.start()
 
+    def clear(c, carry):
+        for t in tabs:
+            t[pl.ds(pl.multiple_of(c * 64, 64), 64), :] = jnp.zeros((64, columns), F32)
+        return carry
+    lax.fori_loop(0, owned // 64, clear, 0)
+    copy.wait()
+
     def add(d, carry):
+        rows = gf.at[pl.ds(d * rows_in, rows_in), :]
         for i in range(0, cap, TABLES):
-            at = [pl.ds(idx_s[d, i + k], 1) for k in range(TABLES)]
-            new = [tabs[k][at[k], :] + gf[pl.ds(d * rows_in + i + k, 1), :] for k in range(TABLES)]
+            at = [pl.ds(idx_s[i + k][d], 1) for k in range(TABLES)]
+            new = [tabs[k][at[k], :] + rows[i + k:i + k + 1, :] for k in range(TABLES)]
             for k in range(TABLES):
                 tabs[k][at[k], :] = new[k]
         return carry
     lax.fori_loop(0, devices, add, 0)
+    load_state.wait()
+
+    eye = iota((LANES, LANES), 0) == iota((LANES, LANES), 1)
+    per = 8
+
+    def measure(c, carry):
+        means = []
+        for k in range(per):
+            rows = pl.ds(pl.multiple_of((c * per + k) * LANES, LANES), LANES)
+            total = (t0[rows, :] + t1[rows, :]) + (t2[rows, :] + t3[rows, :])
+            t0[rows, :] = total
+            square = total * total
+            if k % 2:
+                mean = jnp.sum(square, axis=1, keepdims=True)
+                means.append(jnp.sum(jnp.where(eye, mean, 0.0), axis=0, keepdims=True))
+            else:
+                high = square.astype(BF16)
+                low = (square - high.astype(F32)).astype(BF16)
+                both = lax.dot_general(
+                    jnp.ones((8, 2 * columns), BF16), jnp.concatenate([high, low], axis=1),
+                    (((1,), (1,)), ((), ())), preferred_element_type=F32,
+                )
+                means.append(both[0:1, :])
+        here = pl.ds(pl.multiple_of(c * per, per), per)
+        state = state_ref[here, :] + jnp.concatenate(means, axis=0) * (1.0 / columns)
+        nstate[here, :] = state
+        scales[here, :] = 0.5 / jnp.sqrt(state)
+        return carry
+    lax.fori_loop(0, owned // (per * LANES), measure, 0)
+    out_state = pltpu.make_async_copy(nstate, nstate_hbm, sems.at[3])
+    out_state.start()
     load.wait()
-    load_state.wait()
-
-    ones = jnp.ones((8, columns), BF16)
-    per = 4
-    nt = (((1,), (1,)), ((), ()))
-
+
+    cols_v[:, 0:owned // LANES] = jnp.transpose(scales[...])
     def update(c, carry):
-        rows = pl.ds(pl.multiple_of(c * per * LANES, per * LANES), per * LANES)
-        total = (t0[rows, :] + t1[rows, :]) + (t2[rows, :] + t3[rows, :])
-        square = total * total
-        high = square.astype(BF16)
-        low = (square - high.astype(F32)).astype(BF16)
-        mean = (lax.dot_general(ones, high, nt, preferred_element_type=F32)
-                + lax.dot_general(ones, low, nt, preferred_element_type=F32)) * (1.0 / columns)
-        for k in range(per):
-            state = state_ref[pl.ds(c * per + k, 1), :] + mean[0:1, k * LANES:(k + 1) * LANES]
-            nstate_ref[pl.ds(c * per + k, 1), :] = state
-            scale = jnp.transpose(jnp.broadcast_to(0.5 / jnp.sqrt(state), (LANES, LANES)))
-            here = pl.ds(pl.multiple_of((c * per + k) * LANES, LANES), LANES)
-            emb[here, :] = emb[here, :] - total[k * LANES:(k + 1) * LANES, :] * scale
+        for k in range(8):
+            rows = pl.ds(pl.multiple_of((c * 8 + k) * LANES, LANES), LANES)
+            emb[rows, :] = emb[rows, :] - t0[rows, :] * pick(cols_v[...], c * 8 + k)
+        rows = pl.ds(pl.multiple_of(c * 8 * LANES, 8 * LANES), 8 * LANES)
         pltpu.make_async_copy(emb.at[rows, :], nemb_hbm.at[rows, :], sems.at[2]).start()
         return carry
-    lax.fori_loop(0, owned // (per * LANES), update, 0)
+    lax.fori_loop(0, owned // (8 * LANES), update, 0)
 
     def fetch(d, carry):
+        rows = gf.at[pl.ds(pl.multiple_of(d * cap, cap), cap), :]
         for i in range(cap):
-            gf[pl.ds(d * cap + i, 1), :] = emb[pl.ds(idx_s[d, 2 * cap + i], 1), :]
+            rows[i:i + 1, :] = emb[pl.ds(idx_s[cap + i][d], 1), :]
         return carry
     lax.fori_loop(0, devices, fetch, 0)
-
     ret_ref[...] = gf[0:devices * cap, :].astype(BF16)
+    out_state.wait()
     pltpu.make_async_copy(emb, nemb_hbm, sems.at[2]).wait()
 
 
@@ -149,10 +176,11 @@
     copy.wait()
 
     def take(b, carry):
+        here = rows.at[pl.ds(pl.multiple_of(b * LANES, LANES), LANES), :]
         for j in range(LANES):
-            rows[pl.ds(b * LANES + j, 1), :] = wide[pl.ds(q_ref[b, j], 1), :]
-        return carry
-    lax.fori_loop(0, q_ref.shape[0], take, 0)
+            here[j:j + 1, :] = wide[pl.ds(q_ref.at[j][b], 1), :]
+        return carry
+    lax.fori_loop(0, out_ref.shape[0] // LANES, take, 0)
     out_ref[...] = rows[...].astype(BF16)
 
 
@@ -173,7 +201,7 @@
 
     outgoing, q = pl.pallas_call(
         functools.partial(pack_kernel, cap, rows_out),
-        out_shape=(shape((devices * rows_out, columns), BF16), shape((blocks, LANES), I32)),
+        out_shape=(shape((devices * rows_out, columns), BF16), shape((LANES, LANES), I32)),
         in_specs=[ANY] * 5,
         out_specs=(VM, VM),
         scratch_shapes=[pltpu.VMEM((blocks, LANES), I32)] * 4
@@ -181,8 +209,8 @@
             pltpu.VMEM((lookups, columns), BF16),
             pltpu.VMEM((lookups, columns), F32),
             pltpu.VMEM((devices * rows_out, columns), F32),
-            pltpu.VMEM((blocks, LANES), I32),
-            pltpu.SMEM((blocks, LANES), I32),
+            pltpu.VMEM((LANES, LANES), I32),
+            pltpu.SMEM((LANES, LANES), I32),
             pltpu.SemaphoreType.DMA((6,)),
         ],
         compiler_params=pltpu.CompilerParams(vmem_limit_bytes=12 << 20),
@@ -204,16 +232,18 @@
             shape((devices * cap, columns), BF16),
         ),
         in_specs=[VM, ANY, ANY],
-        out_specs=(ANY, VM, VM),
+        out_specs=(ANY, ANY, VM),
         scratch_shapes=[pltpu.VMEM((owned, columns), F32)] * TABLES
         + [
             pltpu.VMEM((devices * rows_out, columns), F32),
-            pltpu.VMEM((devices, LANES), I32),
-            pltpu.SMEM((devices, LANES), I32),
+            pltpu.VMEM((LANES, devices), I32),
+            pltpu.VMEM((LANES, LANES), F32),
             pltpu.VMEM((owned, columns), F32),
             pltpu.VMEM((owned // LANES, LANES), F32),
+            pltpu.VMEM((owned // LANES, LANES), F32),
+            pltpu.VMEM((owned // LANES, LANES), F32),
             pltpu.SemaphoreType.DMA((4,)),
-        ],
+        ] + [pltpu.SMEM((LANES, devices), I32)],
         compiler_params=pltpu.CompilerParams(vmem_limit_bytes=36 << 20),
         name="owner",
     )(incoming, in_hbm(adagrad_state.reshape(owned // LANES, LANES)), in_hbm(embedding))
@@ -230,7 +260,7 @@
         scratch_shapes=[
             pltpu.VMEM((devices * cap, columns), F32),
             pltpu.VMEM((lookups, columns), F32),
-            pltpu.SMEM((blocks, LANES), I32),
+            pltpu.SMEM((LANES, LANES), I32),
             pltpu.SemaphoreType.DMA,
         ],
         compiler_params=pltpu.CompilerParams(vmem_limit_bytes=12 << 20),

time: 80.5 us -> 75.3 us (0.935)
  Pallas kernels: 25.2 us -> 20.5 us
    pallas_call x1, Pallas kernels: 19.8 us -> 13.8 us  [on_device(): pl.pallas_call(functools.partial(owner_kernel, cap, rows_out), out_shape=...]
where the time goes in v3:
time: 75.3 us; the launch traced here: 75.2 us
  blocking collectives  54 us (72%)
  Pallas kernels  20.5 us (27%)
    all_to_all x1, blocking collectives, exchange(): x = lax.all_to_all(x, AXES, split_axis=0, concat_axis=0, tiled=True)  30.8 us
    all_to_all x1, blocking collectives, on_device(): lax.all_to_all(fetched.reshape(devices, cap, columns), AXES, split_axis=0...  23.3 us
    pallas_call x1, Pallas kernels, on_device(): pl.pallas_call(functools.partial(owner_kernel, cap, rows_out), out_shape=...  13.8 us
    pallas_call x1, Pallas kernels, on_device(): pl.pallas_call(functools.partial(pack_kernel, cap, rows_out), out_shape=(...  3.76 us
    pallas_call x1, Pallas kernels, on_device(): pl.pallas_call(unpack_kernel, out_shape=shape((lookups, columns), BF16),...  2.93 us

profile of v3, /device:TPU:1, one launch (start us, length us, event | category | flops | bytes accessed | tf_op | source)
XLA Modules:
  0.0 75.2 jit_solution(9762898934578625592)
XLA Ops:
  0.6 3.8 %pack.1 = (bf16[4352,128]{1,0:T(8,128)(2,1)S(1)}, s32[128,128]{1,0:T(8,128)S(1)}) custom-call(s32[8,128]{1,0:T(8,128)} %bitcast.15, s32[8,128]{1,0:T(8,128)} %bitcast.16, s32[8,128]{1,0:T(8,128)} %bitcast.17, s32[8,128]{1,0:T(8,128)} %bitcast.18, bf16[1024,128]{1,0:T(8,128)(2,1)} %g_hbm.1), custom_call_target="tpu_custom_call" | custom-call | tf_op jit(solution)/shard_map/pack/pallas_call | solution.py:202
  4.4 30.8 %all_to_all.10 = bf16[128,17,2,128]{3,2,1,0:T(2,128)(2,1)S(1)} all-to-all(bf16[128,17,2,128]{3,2,1,0:T(2,128)(2,1)S(1)} %bitcast.12), channel_id=1, replica_groups=mesh['dp'=4,'rows'=32] {'dp','rows'}, dimensions={0} | all-to-all | bytes 2228224 | tf_op jit(solution)/shard_map/all_to_all | solution.py:222
  35.2 13.8 %owner.1 = (f32[8192,128]{1,0:T(8,128)}, f32[64,128]{1,0:T(8,128)}, bf16[4096,128]{1,0:T(8,128)(2,1)S(1)}) custom-call(bf16[4352,128]{1,0:T(8,128)(2,1)S(1)} %bitcast.10, f32[64,128]{1,0:T(8,128)} %bitcast.14, f32[8192,128]{1,0:T(8,128)} %emb_hbm.1), custom_call_target="tpu_custom_call" | custom-call | tf_op jit(solution)/shard_map/owner/pallas_call | solution.py:227
  49.0 23.3 %all_to_all.11 = bf16[128,32,128]{2,1,0:T(8,128)(2,1)S(1)} all-to-all(bf16[128,32,128]{2,1,0:T(8,128)(2,1)S(1)} %bitcast.13), channel_id=1, replica_groups=mesh['dp'=4,'rows'=32] {'dp','rows'}, dimensions={0} | all-to-all | bytes 2097152 | tf_op jit(solution)/shard_map/all_to_all | solution.py:251
  72.2 2.9 %unpack.1 = bf16[1024,128]{1,0:T(8,128)(2,1)} custom-call(s32[128,128]{1,0:T(8,128)S(1)} %get-tuple-element.11.q_any, bf16[4096,128]{1,0:T(8,128)(2,1)S(1)} %bitcast.11), custom_call_target="tpu_custom_call" | custom-call | tf_op jit(solution)/shard_map/unpack/pallas_call | solution.py:255

commit v4 on v3

--- a/solution.py
+++ b/solution.py
@@ -30,8 +30,9 @@
     outf[...] = jnp.zeros_like(outf)
     blocks = own_ref.shape[0]
     devices = out_ref.shape[0] // rows_out
-    before = (iota((LANES, LANES), 0) < iota((LANES, LANES), 1)).astype(BF16)
-    ones = jnp.ones((LANES, LANES), BF16)
+    counts = jnp.concatenate(
+        [(iota((LANES, LANES), 0) < iota((LANES, LANES), 1)).astype(BF16), jnp.ones((LANES, LANES), BF16)], axis=1
+    )
     row = iota((LANES, LANES), 0)
     meta = jnp.zeros((devices, LANES), F32)
 
@@ -42,9 +43,10 @@
             own = o_ref[b:b + 1, :]
             hit = iota((devices, LANES), 0) == own
             hot = hit.astype(BF16)
-            ahead = jnp.dot(hot, before, preferred_element_type=F32) + base
+            count = jnp.dot(hot, counts, preferred_element_type=F32)
+            ahead = count[:, 0:LANES] + base
             slot = jnp.sum(jnp.where(hit, ahead, 0.0), axis=0, keepdims=True).astype(I32)
-            base = base + jnp.dot(hot, ones, preferred_element_type=F32)
+            base = base + count[:, LANES:]
             off = f_ref[b:b + 1, :]
             value = jnp.where(row < first + cap, off // LANES + 1, off % LANES)
             here = (row >= first) & (row < first + 2 * cap) & (row % cap == slot)
@@ -56,21 +58,23 @@
     loads[0].wait()
     loads[1].wait()
     got, meta = slots(own_ref, off_ref, 0, meta)
-    pos_v[:, 0:blocks] = jnp.transpose(jnp.concatenate([own * rows_out + slot for own, slot in got], axis=0))
+    for b, (own, slot) in enumerate(got):
+        pos_v[b:b + 1, :] = own * rows_out + slot
     copy = pltpu.make_async_copy(pos_v, pos_s, sems.at[5])
     copy.start()
     for load in loads[2:]:
         load.wait()
     gf[...] = g_ref[...].astype(F32)
     got, meta = slots(nown_ref, noff_ref, 2 * cap, meta)
-    q_ref[:, 0:blocks] = jnp.transpose(jnp.concatenate([own * cap + slot for own, slot in got], axis=0))
+    for b, (own, slot) in enumerate(got):
+        q_ref[b:b + 1, :] = own * cap + slot
     outf[pl.ds(cap, devices, stride=rows_out), :] = meta
     copy.wait()
 
     def place(b, carry):
         rows = gf.at[pl.ds(pl.multiple_of(b * LANES, LANES), LANES), :]
         for j in range(LANES):
-            outf[pl.ds(pos_s.at[j][b], 1), :] = rows[j:j + 1, :]
+            outf[pl.ds(pos_s[b, j], 1), :] = rows[j:j + 1, :]
         return carry
     lax.fori_loop(0, blocks, place, 0)
     out_ref[...] = outf[...].astype(BF16)
@@ -90,10 +94,13 @@
     index = ((m - 1.0) * LANES + pltpu.roll(m, LANES - cap, 1)).astype(I32)
     apart = iota((devices, LANES), 0) * cap + iota((devices, LANES), 1) % cap
     idx_v[...] = jnp.transpose(jnp.where(index < 0, apart % owned, index))
-    slots = list(range(cap)) + list(range(2 * cap, 3 * cap))
-    copy = pltpu.make_async_copy(idx_v, idx_all, sems.at[1])
-    copy.start()
-    idx_s = [idx_all.at[i] for i in slots]
+    copies = [
+        pltpu.make_async_copy(idx_v.at[pl.ds(2 * cap * k, cap), :], idx_all.at[pl.ds(cap * k, cap), :], sems.at[k + 4])
+        for k in range(2)
+    ]
+    for copy in copies:
+        copy.start()
+    idx_s = [idx_all.at[i] for i in range(2 * cap)]
     load = pltpu.make_async_copy(emb_hbm, emb, sems.at[0])
     load.start()
     load_state = pltpu.make_async_copy(state_hbm, state_ref, sems.at[3])
@@ -104,7 +111,7 @@
             t[pl.ds(pl.multiple_of(c * 64, 64), 64), :] = jnp.zeros((64, columns), F32)
         return carry
     lax.fori_loop(0, owned // 64, clear, 0)
-    copy.wait()
+    copies[0].wait()
 
     def add(d, carry):
         rows = gf.at[pl.ds(d * rows_in, rows_in), :]
@@ -117,7 +124,6 @@
     lax.fori_loop(0, devices, add, 0)
     load_state.wait()
 
-    eye = iota((LANES, LANES), 0) == iota((LANES, LANES), 1)
     per = 8
 
     def measure(c, carry):
@@ -127,17 +133,13 @@
             total = (t0[rows, :] + t1[rows, :]) + (t2[rows, :] + t3[rows, :])
             t0[rows, :] = total
             square = total * total
-            if k % 2:
-                mean = jnp.sum(square, axis=1, keepdims=True)
-                means.append(jnp.sum(jnp.where(eye, mean, 0.0), axis=0, keepdims=True))
-            else:
-                high = square.astype(BF16)
-                low = (square - high.astype(F32)).astype(BF16)
-                both = lax.dot_general(
-                    jnp.ones((8, 2 * columns), BF16), jnp.concatenate([high, low], axis=1),
-                    (((1,), (1,)), ((), ())), preferred_element_type=F32,
-                )
-                means.append(both[0:1, :])
+            high = square.astype(BF16)
+            low = (square - high.astype(F32)).astype(BF16)
+            both = lax.dot_general(
+                jnp.ones((8, 2 * columns), BF16), jnp.concatenate([high, low], axis=1),
+                (((1,), (1,)), ((), ())), preferred_element_type=F32,
+            )
+            means.append(both[0:1, :])
         here = pl.ds(pl.multiple_of(c * per, per), per)
         state = state_ref[here, :] + jnp.concatenate(means, axis=0) * (1.0 / columns)
         nstate[here, :] = state
@@ -158,6 +160,8 @@
         return carry
     lax.fori_loop(0, owned // (8 * LANES), update, 0)
 
+    copies[1].wait()
+
     def fetch(d, carry):
         rows = gf.at[pl.ds(pl.multiple_of(d * cap, cap), cap), :]
         for i in range(cap):
@@ -169,8 +173,8 @@
     pltpu.make_async_copy(emb, nemb_hbm, sems.at[2]).wait()
 
 
-def unpack_kernel(q_any, ret_ref, out_ref, wide, rows, q_ref, sem):
-    copy = pltpu.make_async_copy(q_any, q_ref, sem)
+def unpack_kernel(q_any, ret_ref, out_hbm, wide, rows, out_ref, q_ref, sems):
+    copy = pltpu.make_async_copy(q_any, q_ref, sems.at[0])
     copy.start()
     wide[...] = ret_ref[...].astype(F32)
     copy.wait()
@@ -178,10 +182,13 @@
     def take(b, carry):
         here = rows.at[pl.ds(pl.multiple_of(b * LANES, LANES), LANES), :]
         for j in range(LANES):
-            here[j:j + 1, :] = wide[pl.ds(q_ref.at[j][b], 1), :]
+            here[j:j + 1, :] = wide[pl.ds(q_ref[b, j], 1), :]
+        block = pl.ds(pl.multiple_of(b * LANES, LANES), LANES)
+        out_ref[block, :] = here[...].astype(BF16)
+        pltpu.make_async_copy(out_ref.at[block, :], out_hbm.at[block, :], sems.at[1]).start()
         return carry
     lax.fori_loop(0, out_ref.shape[0] // LANES, take, 0)
-    out_ref[...] = rows[...].astype(BF16)
+    pltpu.make_async_copy(out_ref, out_hbm, sems.at[1]).wait()
 
 
 VM = pl.BlockSpec(memory_space=pltpu.VMEM)
@@ -201,7 +208,7 @@
 
     outgoing, q = pl.pallas_call(
         functools.partial(pack_kernel, cap, rows_out),
-        out_shape=(shape((devices * rows_out, columns), BF16), shape((LANES, LANES), I32)),
+        out_shape=(shape((devices * rows_out, columns), BF16), shape((blocks, LANES), I32)),
         in_specs=[ANY] * 5,
         out_specs=(VM, VM),
         scratch_shapes=[pltpu.VMEM((blocks, LANES), I32)] * 4
@@ -209,8 +216,8 @@
             pltpu.VMEM((lookups, columns), BF16),
             pltpu.VMEM((lookups, columns), F32),
             pltpu.VMEM((devices * rows_out, columns), F32),
-            pltpu.VMEM((LANES, LANES), I32),
-            pltpu.SMEM((LANES, LANES), I32),
+            pltpu.VMEM((blocks, LANES), I32),
+            pltpu.SMEM((blocks, LANES), I32),
             pltpu.SemaphoreType.DMA((6,)),
         ],
         compiler_params=pltpu.CompilerParams(vmem_limit_bytes=12 << 20),
@@ -242,8 +249,9 @@
             pltpu.VMEM((owned // LANES, LANES), F32),
             pltpu.VMEM((owned // LANES, LANES), F32),
             pltpu.VMEM((owned // LANES, LANES), F32),
-            pltpu.SemaphoreType.DMA((4,)),
-        ] + [pltpu.SMEM((LANES, devices), I32)],
+            pltpu.SemaphoreType.DMA((6,)),
+            pltpu.SMEM((2 * cap, devices), I32),
+        ],
         compiler_params=pltpu.CompilerParams(vmem_limit_bytes=36 << 20),
         name="owner",
     )(incoming, in_hbm(adagrad_state.reshape(owned // LANES, LANES)), in_hbm(embedding))
@@ -256,12 +264,13 @@
         unpack_kernel,
         out_shape=shape((lookups, columns), BF16),
         in_specs=[ANY, VM],
-        out_specs=VM,
+        out_specs=ANY,
         scratch_shapes=[
             pltpu.VMEM((devices * cap, columns), F32),
             pltpu.VMEM((lookups, columns), F32),
-            pltpu.SMEM((LANES, LANES), I32),
-            pltpu.SemaphoreType.DMA,
+            pltpu.VMEM((lookups, columns), BF16),
+            pltpu.SMEM((blocks, LANES), I32),
+            pltpu.SemaphoreType.DMA((2,)),
         ],
         compiler_params=pltpu.CompilerParams(vmem_limit_bytes=12 << 20),
         name="unpack",

time: 75.3 us -> 73.9 us (0.981)
  Pallas kernels: 20.5 us -> 19 us
where the time goes in v4:
time: 73.9 us; the launch traced here: 73.7 us
  blocking collectives  54 us (73%)
  Pallas kernels  19 us (26%)
    all_to_all x1, blocking collectives, exchange(): x = lax.all_to_all(x, AXES, split_axis=0, concat_axis=0, tiled=True)  30.8 us
    all_to_all x1, blocking collectives, on_device(): lax.all_to_all(fetched.reshape(devices, cap, columns), AXES, split_axis=0...  23.3 us
    pallas_call x1, Pallas kernels, on_device(): pl.pallas_call(functools.partial(owner_kernel, cap, rows_out), out_shape=...  13.7 us
    pallas_call x1, Pallas kernels, on_device(): pl.pallas_call(functools.partial(pack_kernel, cap, rows_out), out_shape=(...  3.13 us
    pallas_call x1, Pallas kernels, on_device(): pl.pallas_call(unpack_kernel, out_shape=shape((lookups, columns), BF16),...  2.19 us

profile of v4, /device:TPU:1, one launch (start us, length us, event | category | flops | bytes accessed | tf_op | source)
XLA Modules:
  0.0 73.7 jit_solution(9866828532027357555)
XLA Ops:
  0.6 3.1 %pack.1 = (bf16[4352,128]{1,0:T(8,128)(2,1)S(1)}, s32[8,128]{1,0:T(8,128)S(1)}) custom-call(s32[8,128]{1,0:T(8,128)} %bitcast.15, s32[8,128]{1,0:T(8,128)} %bitcast.16, s32[8,128]{1,0:T(8,128)} %bitcast.17, s32[8,128]{1,0:T(8,128)} %bitcast.18, bf16[1024,128]{1,0:T(8,128)(2,1)} %g_hbm.1), custom_call_target="tpu_custom_call" | custom-call | tf_op jit(solution)/shard_map/pack/pallas_call | solution.py:209
  3.8 30.8 %all_to_all.10 = bf16[128,17,2,128]{3,2,1,0:T(2,128)(2,1)S(1)} all-to-all(bf16[128,17,2,128]{3,2,1,0:T(2,128)(2,1)S(1)} %bitcast.12), channel_id=1, replica_groups=mesh['dp'=4,'rows'=32] {'dp','rows'}, dimensions={0} | all-to-all | bytes 2228224 | tf_op jit(solution)/shard_map/all_to_all | solution.py:229
  34.5 13.7 %owner.1 = (f32[8192,128]{1,0:T(8,128)}, f32[64,128]{1,0:T(8,128)}, bf16[4096,128]{1,0:T(8,128)(2,1)S(1)}) custom-call(bf16[4352,128]{1,0:T(8,128)(2,1)S(1)} %bitcast.10, f32[64,128]{1,0:T(8,128)} %bitcast.14, f32[8192,128]{1,0:T(8,128)} %emb_hbm.1), custom_call_target="tpu_custom_call" | custom-call | tf_op jit(solution)/shard_map/owner/pallas_call | solution.py:234
  48.2 23.3 %all_to_all.11 = bf16[128,32,128]{2,1,0:T(8,128)(2,1)S(1)} all-to-all(bf16[128,32,128]{2,1,0:T(8,128)(2,1)S(1)} %bitcast.13), channel_id=1, replica_groups=mesh['dp'=4,'rows'=32] {'dp','rows'}, dimensions={0} | all-to-all | bytes 2097152 | tf_op jit(solution)/shard_map/all_to_all | solution.py:259
  71.5 2.2 %unpack.1 = bf16[1024,128]{1,0:T(8,128)(2,1)} custom-call(s32[8,128]{1,0:T(8,128)S(1)} %get-tuple-element.11.q_any, bf16[4096,128]{1,0:T(8,128)(2,1)S(1)} %bitcast.11), custom_call_target="tpu_custom_call" | custom-call | tf_op jit(solution)/shard_map/unpack/pallas_call | solution.py:263

commit v5 on v4

--- a/solution.py
+++ b/solution.py
@@ -18,7 +18,9 @@
 
 
 def pack_kernel(cap, rows_out, own_hbm, off_hbm, nown_hbm, noff_hbm, g_hbm, out_ref, q_ref,
-                own_ref, off_ref, nown_ref, noff_ref, g_ref, gf, outf, pos_v, pos_s, sems):
+                t0, t1, t2, t3, own_ref, off_ref, nown_ref, noff_ref, g_ref, gf, outf, pos_v, pos_s, sems):
+    blocks = own_ref.shape[0]
+    devices = out_ref.shape[0] // rows_out
     loads = [
         pltpu.make_async_copy(src, dst, sems.at[k])
         for k, (src, dst) in enumerate((
@@ -28,47 +30,49 @@
     for load in loads:
         load.start()
     outf[...] = jnp.zeros_like(outf)
-    blocks = own_ref.shape[0]
-    devices = out_ref.shape[0] // rows_out
+
+    def clear(tabs):
+        def step(c, carry):
+            for t in tabs:
+                t[pl.ds(pl.multiple_of(c * 128, 128), 128), :] = jnp.zeros((128, t.shape[1]), F32)
+            return carry
+        lax.fori_loop(0, t0.shape[0] // 128, step, 0)
+
+    clear((t0, t1))
     counts = jnp.concatenate(
         [(iota((LANES, LANES), 0) < iota((LANES, LANES), 1)).astype(BF16), jnp.ones((LANES, LANES), BF16)], axis=1
     )
-    row = iota((LANES, LANES), 0)
-    meta = jnp.zeros((devices, LANES), F32)
-
-    def slots(o_ref, f_ref, first, meta):
-        base = jnp.zeros((devices, LANES), F32)
-        out = []
-        for b in range(blocks):
-            own = o_ref[b:b + 1, :]
-            hit = iota((devices, LANES), 0) == own
+    row = iota((cap, LANES), 0)
+    bases = [jnp.zeros((devices, LANES), F32)] * 2
+    metas = [jnp.zeros((devices, 2 * cap), F32)] * 2
+    for load in loads[:4]:
+        load.wait()
+    for b in range(blocks):
+        for n, (o_ref, f_ref) in enumerate(((own_ref, off_ref), (nown_ref, noff_ref))):
+            own, off = o_ref[b:b + 1, :], f_ref[b:b + 1, :]
+            hit = jnp.where(iota((devices, LANES), 0) == own, 1.0, 0.0)
             hot = hit.astype(BF16)
             count = jnp.dot(hot, counts, preferred_element_type=F32)
-            ahead = count[:, 0:LANES] + base
-            slot = jnp.sum(jnp.where(hit, ahead, 0.0), axis=0, keepdims=True).astype(I32)
-            base = base + count[:, LANES:]
-            off = f_ref[b:b + 1, :]
-            value = jnp.where(row < first + cap, off // LANES + 1, off % LANES)
-            here = (row >= first) & (row < first + 2 * cap) & (row % cap == slot)
-            sel = jnp.where(here, value, 0).astype(F32).astype(BF16)
-            meta = meta + lax.dot_general(hot, sel, (((1,), (1,)), ((), ())), preferred_element_type=F32)
-            out.append((own, slot))
-        return out, meta
-
-    loads[0].wait()
-    loads[1].wait()
-    got, meta = slots(own_ref, off_ref, 0, meta)
-    for b, (own, slot) in enumerate(got):
-        pos_v[b:b + 1, :] = own * rows_out + slot
+            ahead = count[:, 0:LANES] + bases[n]
+            slot = jnp.sum(hit * ahead, axis=0, keepdims=True).astype(I32)
+            bases[n] = bases[n] + count[:, LANES:]
+            values = (off // LANES + 1, off % LANES)
+            sel = jnp.concatenate(
+                [jnp.where(row == slot, value.astype(F32), 0.0) for value in values], axis=0
+            ).astype(BF16)
+            metas[n] = metas[n] + lax.dot_general(
+                hot, sel, (((1,), (1,)), ((), ())), preferred_element_type=F32
+            )
+            if n == 0:
+                pos_v[b:b + 1, :] = own * rows_out + slot
+            else:
+                q_ref[b:b + 1, :] = own * cap + slot
     copy = pltpu.make_async_copy(pos_v, pos_s, sems.at[5])
     copy.start()
-    for load in loads[2:]:
-        load.wait()
+    outf[pl.ds(cap, devices, stride=rows_out), :] = jnp.concatenate(metas, axis=1)
+    loads[4].wait()
     gf[...] = g_ref[...].astype(F32)
-    got, meta = slots(nown_ref, noff_ref, 2 * cap, meta)
-    for b, (own, slot) in enumerate(got):
-        q_ref[b:b + 1, :] = own * cap + slot
-    outf[pl.ds(cap, devices, stride=rows_out), :] = meta
+    clear((t2, t3))
     copy.wait()
 
     def place(b, carry):
@@ -84,7 +88,7 @@
     return jnp.take_along_axis(x, jnp.full(x.shape, lane, I32), axis=1)
 
 
-def owner_kernel(cap, rows_in, inc_ref, state_hbm, emb_hbm, nemb_hbm, nstate_hbm, ret_ref,
+def owner_kernel(cap, rows_in, inc_ref, state_hbm, emb_hbm, _0, _1, _2, _3, nemb_hbm, nstate_hbm, ret_ref,
                  t0, t1, t2, t3, gf, idx_v, cols_v, emb, state_ref, nstate, scales, sems, idx_all):
     devices = idx_v.shape[1]
     owned, columns = emb.shape
@@ -106,11 +110,6 @@
     load_state = pltpu.make_async_copy(state_hbm, state_ref, sems.at[3])
     load_state.start()
 
-    def clear(c, carry):
-        for t in tabs:
-            t[pl.ds(pl.multiple_of(c * 64, 64), 64), :] = jnp.zeros((64, columns), F32)
-        return carry
-    lax.fori_loop(0, owned // 64, clear, 0)
     copies[0].wait()
 
     def add(d, carry):
@@ -162,13 +161,18 @@
 
     copies[1].wait()
 
+    def narrow(d):
+        rows = pl.ds(pl.multiple_of(d * cap, cap), cap)
+        ret_ref[rows, :] = gf[rows, :].astype(BF16)
+
     def fetch(d, carry):
         rows = gf.at[pl.ds(pl.multiple_of(d * cap, cap), cap), :]
         for i in range(cap):
             rows[i:i + 1, :] = emb[pl.ds(idx_s[cap + i][d], 1), :]
+        narrow(jnp.maximum(d - 1, 0))
         return carry
     lax.fori_loop(0, devices, fetch, 0)
-    ret_ref[...] = gf[0:devices * cap, :].astype(BF16)
+    narrow(devices - 1)
     out_state.wait()
     pltpu.make_async_copy(emb, nemb_hbm, sems.at[2]).wait()
 
@@ -206,11 +210,13 @@
     view = lambda x: x.reshape(blocks, LANES)
     in_hbm = lambda x: pltpu.with_memory_space_constraint(x, pltpu.HBM)
 
-    outgoing, q = pl.pallas_call(
+    table = pltpu.VMEM((owned, columns), F32)
+    outgoing, q, *tables = pl.pallas_call(
         functools.partial(pack_kernel, cap, rows_out),
-        out_shape=(shape((devices * rows_out, columns), BF16), shape((blocks, LANES), I32)),
+        out_shape=(shape((devices * rows_out, columns), BF16), shape((blocks, LANES), I32))
+        + (table,) * TABLES,
         in_specs=[ANY] * 5,
-        out_specs=(VM, VM),
+        out_specs=(VM,) * (2 + TABLES),
         scratch_shapes=[pltpu.VMEM((blocks, LANES), I32)] * 4
         + [
             pltpu.VMEM((lookups, columns), BF16),
@@ -237,11 +243,10 @@
             shape(embedding.shape, F32),
             shape((owned // LANES, LANES), F32),
             shape((devices * cap, columns), BF16),
-        ),
-        in_specs=[VM, ANY, ANY],
-        out_specs=(ANY, ANY, VM),
-        scratch_shapes=[pltpu.VMEM((owned, columns), F32)] * TABLES
-        + [
+        ) + (table,) * TABLES,
+        in_specs=[VM, ANY, ANY] + [VM] * TABLES,
+        out_specs=(ANY, ANY, VM) + (VM,) * TABLES,
+        scratch_shapes=[
             pltpu.VMEM((devices * rows_out, columns), F32),
             pltpu.VMEM((LANES, devices), I32),
             pltpu.VMEM((LANES, LANES), F32),
@@ -252,9 +257,11 @@
             pltpu.SemaphoreType.DMA((6,)),
             pltpu.SMEM((2 * cap, devices), I32),
         ],
-        compiler_params=pltpu.CompilerParams(vmem_limit_bytes=36 << 20),
+        input_output_aliases={3 + k: 3 + k for k in range(TABLES)},
+        compiler_params=pltpu.CompilerParams(vmem_limit_bytes=16 << 20),
         name="owner",
-    )(incoming, in_hbm(adagrad_state.reshape(owned // LANES, LANES)), in_hbm(embedding))
+    )(incoming, in_hbm(adagrad_state.reshape(owned // LANES, LANES)), in_hbm(embedding),
+      *[pltpu.with_memory_space_constraint(t, pltpu.VMEM) for t in tables])[:3]
 
     returned = lax.all_to_all(
         fetched.reshape(devices, cap, columns), AXES, split_axis=0, concat_axis=0, tiled=True

time: 73.9 us -> 74.7 us (1.011)
  Pallas kernels: 19 us -> 19.9 us
where the time goes in v5:
time: 74.7 us; the launch traced here: 74.6 us
  blocking collectives  54 us (72%)
  Pallas kernels  19.9 us (27%)
    all_to_all x1, blocking collectives, exchange(): x = lax.all_to_all(x, AXES, split_axis=0, concat_axis=0, tiled=True)  30.8 us
    all_to_all x1, blocking collectives, on_device(): lax.all_to_all(fetched.reshape(devices, cap, columns), AXES, split_axis=0...  23.3 us
    pallas_call x1, Pallas kernels, on_device(): pl.pallas_call(functools.partial(owner_kernel, cap, rows_out), out_shape=...  14.1 us
    pallas_call x1, Pallas kernels, on_device(): pl.pallas_call(functools.partial(pack_kernel, cap, rows_out), out_shape=(...  3.66 us
    pallas_call x1, Pallas kernels, on_device(): pl.pallas_call(unpack_kernel, out_shape=shape((lookups, columns), BF16),...  2.19 us

profile of v5, /device:TPU:1, one launch (start us, length us, event | category | flops | bytes accessed | tf_op | source)
XLA Modules:
  0.0 74.6 jit_solution(1124336198175547514)
XLA Ops:
  0.6 3.7 %pack.1 = (bf16[4352,128]{1,0:T(8,128)(2,1)S(1)}, s32[8,128]{1,0:T(8,128)S(1)}, f32[8192,128]{1,0:T(8,128)S(1)}, f32[8192,128]{1,0:T(8,128)S(1)}, f32[8192,128]{1,0:T(8,128)S(1)}, /*index=5*/f32[8192,128]{1,0:T(8,128)S(1)}) custom-call(s32[8,128]{1,0:T(8,128)} %bitcast.15, s32[8,128]{1,0:T(8,128)} %bitcast.16, s32[8,128]{1,0:T(8,128)} %bitcast.17, ...), custom_call_target="tpu_custom_call" | custom-call | tf_op jit(solution)/shard_map/pack/pallas_call | solution.py:214
  4.3 30.8 %all_to_all.10 = bf16[128,17,2,128]{3,2,1,0:T(2,128)(2,1)S(1)} all-to-all(bf16[128,17,2,128]{3,2,1,0:T(2,128)(2,1)S(1)} %bitcast.12), channel_id=1, replica_groups=mesh['dp'=4,'rows'=32] {'dp','rows'}, dimensions={0} | all-to-all | bytes 2228224 | tf_op jit(solution)/shard_map/all_to_all | solution.py:235
  35.1 14.1 %owner.1 = (f32[8192,128]{1,0:T(8,128)}, f32[64,128]{1,0:T(8,128)}, bf16[4096,128]{1,0:T(8,128)(2,1)S(1)}, f32[8192,128]{1,0:T(8,128)S(1)}, f32[8192,128]{1,0:T(...) custom-call(bf16[4352,128]{1,0:T(8,128)(2,1)S(1)} %bitcast.10, ...), custom_call_target="tpu_custom_call", output_to_operand_aliasing={{3}: (3, {}), {4}: (4, {}), {5}: (5, {}), {6}: (6, {})} | custom-call | tf_op jit(solution)/shard_map/owner/pallas_call | solution.py:240
  49.1 23.3 %all_to_all.11 = bf16[128,32,128]{2,1,0:T(8,128)(2,1)S(1)} all-to-all(bf16[128,32,128]{2,1,0:T(8,128)(2,1)S(1)} %bitcast.13), channel_id=1, replica_groups=mesh['dp'=4,'rows'=32] {'dp','rows'}, dimensions={0} | all-to-all | bytes 2097152 | tf_op jit(solution)/shard_map/all_to_all | solution.py:266
  72.4 2.2 %unpack.1 = bf16[1024,128]{1,0:T(8,128)(2,1)} custom-call(s32[8,128]{1,0:T(8,128)S(1)} %get-tuple-element.19.q_any, bf16[4096,128]{1,0:T(8,128)(2,1)S(1)} %bitcast.11), custom_call_target="tpu_custom_call" | custom-call | tf_op jit(solution)/shard_map/unpack/pallas_call | solution.py:270

commit v6 on v4

--- a/solution.py
+++ b/solution.py
@@ -33,31 +33,34 @@
     counts = jnp.concatenate(
         [(iota((LANES, LANES), 0) < iota((LANES, LANES), 1)).astype(BF16), jnp.ones((LANES, LANES), BF16)], axis=1
     )
-    row = iota((LANES, LANES), 0)
-    meta = jnp.zeros((devices, LANES), F32)
-
-    def slots(o_ref, f_ref, first, meta):
+    row = iota((2 * cap, LANES), 0)
+    name = iota((devices, LANES), 0).astype(F32).astype(BF16)
+
+    def slots(o_ref, f_ref):
         base = jnp.zeros((devices, LANES), F32)
-        out = []
+        out, hots, sels = [], [], []
         for b in range(blocks):
             own = o_ref[b:b + 1, :]
-            hit = iota((devices, LANES), 0) == own
-            hot = hit.astype(BF16)
+            hot = jnp.where(name == own.astype(F32).astype(BF16), jnp.bfloat16(1), jnp.bfloat16(0))
             count = jnp.dot(hot, counts, preferred_element_type=F32)
-            ahead = count[:, 0:LANES] + base
-            slot = jnp.sum(jnp.where(hit, ahead, 0.0), axis=0, keepdims=True).astype(I32)
+            ahead = (count[:, 0:LANES] + base).astype(BF16)
+            slot = jnp.sum((hot * ahead).astype(F32), axis=0, keepdims=True).astype(I32)
             base = base + count[:, LANES:]
             off = f_ref[b:b + 1, :]
-            value = jnp.where(row < first + cap, off // LANES + 1, off % LANES)
-            here = (row >= first) & (row < first + 2 * cap) & (row % cap == slot)
-            sel = jnp.where(here, value, 0).astype(F32).astype(BF16)
-            meta = meta + lax.dot_general(hot, sel, (((1,), (1,)), ((), ())), preferred_element_type=F32)
+            value = jnp.where(row < cap, off // LANES + 1, off % LANES)
+            sel = jnp.where(row % cap == slot, value, 0).astype(F32).astype(BF16)
+            hots.append(hot)
+            sels.append(sel)
             out.append((own, slot))
+        meta = lax.dot_general(
+            jnp.concatenate(hots, axis=1), jnp.concatenate(sels, axis=1), (((1,), (1,)), ((), ())),
+            preferred_element_type=F32,
+        )
         return out, meta
 
     loads[0].wait()
     loads[1].wait()
-    got, meta = slots(own_ref, off_ref, 0, meta)
+    got, sent = slots(own_ref, off_ref)
     for b, (own, slot) in enumerate(got):
         pos_v[b:b + 1, :] = own * rows_out + slot
     copy = pltpu.make_async_copy(pos_v, pos_s, sems.at[5])
@@ -65,18 +68,18 @@
     for load in loads[2:]:
         load.wait()
     gf[...] = g_ref[...].astype(F32)
-    got, meta = slots(nown_ref, noff_ref, 2 * cap, meta)
+    got, asked = slots(nown_ref, noff_ref)
     for b, (own, slot) in enumerate(got):
         q_ref[b:b + 1, :] = own * cap + slot
-    outf[pl.ds(cap, devices, stride=rows_out), :] = meta
+    outf[pl.ds(cap, devices, stride=rows_out), :] = jnp.concatenate([sent, asked], axis=1)
     copy.wait()
 
-    def place(b, carry):
-        rows = gf.at[pl.ds(pl.multiple_of(b * LANES, LANES), LANES), :]
-        for j in range(LANES):
-            outf[pl.ds(pos_s[b, j], 1), :] = rows[j:j + 1, :]
-        return carry
-    lax.fori_loop(0, blocks, place, 0)
+    def place(i, carry):
+        for u in range(16):
+            for b in range(blocks):
+                outf[pl.ds(pos_s.at[b][i * 16 + u], 1), :] = gf[pl.ds(b * LANES + i * 16 + u, 1), :]
+        return carry
+    lax.fori_loop(0, LANES // 16, place, 0)
     out_ref[...] = outf[...].astype(BF16)
 
 
@@ -113,15 +116,17 @@
     lax.fori_loop(0, owned // 64, clear, 0)
     copies[0].wait()
 
-    def add(d, carry):
-        rows = gf.at[pl.ds(d * rows_in, rows_in), :]
-        for i in range(0, cap, TABLES):
-            at = [pl.ds(idx_s[i + k][d], 1) for k in range(TABLES)]
-            new = [tabs[k][at[k], :] + rows[i + k:i + k + 1, :] for k in range(TABLES)]
-            for k in range(TABLES):
-                tabs[k][at[k], :] = new[k]
-        return carry
-    lax.fori_loop(0, devices, add, 0)
+    def add(c, carry):
+        for n in range(8):
+            d = c * 8 + n
+            rows = gf.at[pl.ds(d * rows_in, rows_in), :]
+            for i in range(0, cap, TABLES):
+                at = [pl.ds(idx_s[i + k][d], 1) for k in range(TABLES)]
+                new = [tabs[k][at[k], :] + rows[i + k:i + k + 1, :] for k in range(TABLES)]
+                for k in range(TABLES):
+                    tabs[k][at[k], :] = new[k]
+        return carry
+    lax.fori_loop(0, devices // 8, add, 0)
     load_state.wait()
 
     per = 8
@@ -162,33 +167,32 @@
 
     copies[1].wait()
 
-    def fetch(d, carry):
-        rows = gf.at[pl.ds(pl.multiple_of(d * cap, cap), cap), :]
-        for i in range(cap):
-            rows[i:i + 1, :] = emb[pl.ds(idx_s[cap + i][d], 1), :]
-        return carry
-    lax.fori_loop(0, devices, fetch, 0)
+    def fetch(c, carry):
+        for n in range(8):
+            d = c * 8 + n
+            rows = gf.at[pl.ds(pl.multiple_of(d * cap, cap), cap), :]
+            for i in range(cap):
+                rows[i:i + 1, :] = emb[pl.ds(idx_s[cap + i][d], 1), :]
+        return carry
+    lax.fori_loop(0, devices // 8, fetch, 0)
     ret_ref[...] = gf[0:devices * cap, :].astype(BF16)
     out_state.wait()
     pltpu.make_async_copy(emb, nemb_hbm, sems.at[2]).wait()
 
 
-def unpack_kernel(q_any, ret_ref, out_hbm, wide, rows, out_ref, q_ref, sems):
-    copy = pltpu.make_async_copy(q_any, q_ref, sems.at[0])
+def unpack_kernel(q_any, ret_ref, out_ref, wide, rows, q_ref, sem):
+    copy = pltpu.make_async_copy(q_any, q_ref, sem)
     copy.start()
     wide[...] = ret_ref[...].astype(F32)
     copy.wait()
 
-    def take(b, carry):
-        here = rows.at[pl.ds(pl.multiple_of(b * LANES, LANES), LANES), :]
-        for j in range(LANES):
-            here[j:j + 1, :] = wide[pl.ds(q_ref[b, j], 1), :]
-        block = pl.ds(pl.multiple_of(b * LANES, LANES), LANES)
-        out_ref[block, :] = here[...].astype(BF16)
-        pltpu.make_async_copy(out_ref.at[block, :], out_hbm.at[block, :], sems.at[1]).start()
-        return carry
-    lax.fori_loop(0, out_ref.shape[0] // LANES, take, 0)
-    pltpu.make_async_copy(out_ref, out_hbm, sems.at[1]).wait()
+    def take(i, carry):
+        for u in range(16):
+            for b in range(q_ref.shape[0]):
+                rows[pl.ds(b * LANES + i * 16 + u, 1), :] = wide[pl.ds(q_ref.at[b][i * 16 + u], 1), :]
+        return carry
+    lax.fori_loop(0, LANES // 16, take, 0)
+    out_ref[...] = rows[...].astype(BF16)
 
 
 VM = pl.BlockSpec(memory_space=pltpu.VMEM)
@@ -264,13 +268,12 @@
         unpack_kernel,
         out_shape=shape((lookups, columns), BF16),
         in_specs=[ANY, VM],
-        out_specs=ANY,
+        out_specs=VM,
         scratch_shapes=[
             pltpu.VMEM((devices * cap, columns), F32),
             pltpu.VMEM((lookups, columns), F32),
-            pltpu.VMEM((lookups, columns), BF16),
             pltpu.SMEM((blocks, LANES), I32),
-            pltpu.SemaphoreType.DMA((2,)),
+            pltpu.SemaphoreType.DMA,
         ],
         compiler_params=pltpu.CompilerParams(vmem_limit_bytes=12 << 20),
         name="unpack",

time: 73.9 us -> 72.2 us (0.977)
  Pallas kernels: 19 us -> 17.4 us
    pallas_call x1, Pallas kernels: 13.7 us -> 12.8 us  [on_device(): pl.pallas_call(functools.partial(owner_kernel, cap, rows_out), out_shape=...]
where the time goes in v6:
time: 72.2 us; the launch traced here: 72.1 us
  blocking collectives  54 us (75%)
  Pallas kernels  17.4 us (24%)
    all_to_all x1, blocking collectives, exchange(): x = lax.all_to_all(x, AXES, split_axis=0, concat_axis=0, tiled=True)  30.8 us
    all_to_all x1, blocking collectives, on_device(): lax.all_to_all(fetched.reshape(devices, cap, columns), AXES, split_axis=0...  23.3 us
    pallas_call x1, Pallas kernels, on_device(): pl.pallas_call(functools.partial(owner_kernel, cap, rows_out), out_shape=...  12.8 us
    pallas_call x1, Pallas kernels, on_device(): pl.pallas_call(functools.partial(pack_kernel, cap, rows_out), out_shape=(...  2.67 us
    pallas_call x1, Pallas kernels, on_device(): pl.pallas_call(unpack_kernel, out_shape=shape((lookups, columns), BF16),...  1.96 us

profile of v6, /device:TPU:1, one launch (start us, length us, event | category | flops | bytes accessed | tf_op | source)
XLA Modules:
  0.0 72.1 jit_solution(6513663826568271534)
XLA Ops:
  0.6 2.7 %pack.1 = (bf16[4352,128]{1,0:T(8,128)(2,1)S(1)}, s32[8,128]{1,0:T(8,128)S(1)}) custom-call(s32[8,128]{1,0:T(8,128)} %bitcast.15, s32[8,128]{1,0:T(8,128)} %bitcast.16, s32[8,128]{1,0:T(8,128)} %bitcast.17, s32[8,128]{1,0:T(8,128)} %bitcast.18, bf16[1024,128]{1,0:T(8,128)(2,1)} %g_hbm.1), custom_call_target="tpu_custom_call" | custom-call | tf_op jit(solution)/shard_map/pack/pallas_call | solution.py:213
  3.3 30.8 %all_to_all.10 = bf16[128,17,2,128]{3,2,1,0:T(2,128)(2,1)S(1)} all-to-all(bf16[128,17,2,128]{3,2,1,0:T(2,128)(2,1)S(1)} %bitcast.12), channel_id=1, replica_groups=mesh['dp'=4,'rows'=32] {'dp','rows'}, dimensions={0} | all-to-all | bytes 2228224 | tf_op jit(solution)/shard_map/all_to_all | solution.py:233
  34.1 12.8 %owner.1 = (f32[8192,128]{1,0:T(8,128)}, f32[64,128]{1,0:T(8,128)}, bf16[4096,128]{1,0:T(8,128)(2,1)S(1)}) custom-call(bf16[4352,128]{1,0:T(8,128)(2,1)S(1)} %bitcast.10, f32[64,128]{1,0:T(8,128)} %bitcast.14, f32[8192,128]{1,0:T(8,128)} %emb_hbm.1), custom_call_target="tpu_custom_call" | custom-call | tf_op jit(solution)/shard_map/owner/pallas_call | solution.py:238
  46.8 23.3 %all_to_all.11 = bf16[128,32,128]{2,1,0:T(8,128)(2,1)S(1)} all-to-all(bf16[128,32,128]{2,1,0:T(8,128)(2,1)S(1)} %bitcast.13), channel_id=1, replica_groups=mesh['dp'=4,'rows'=32] {'dp','rows'}, dimensions={0} | all-to-all | bytes 2097152 | tf_op jit(solution)/shard_map/all_to_all | solution.py:263
  70.1 2.0 %unpack.1 = bf16[1024,128]{1,0:T(8,128)(2,1)} custom-call(s32[8,128]{1,0:T(8,128)S(1)} %get-tuple-element.11.q_any, bf16[4096,128]{1,0:T(8,128)(2,1)S(1)} %bitcast.11), custom_call_target="tpu_custom_call" | custom-call | tf_op jit(solution)/shard_map/unpack/pallas_call | solution.py:267

commit v7 on v6

--- a/solution.py
+++ b/solution.py
@@ -88,10 +88,9 @@
 
 
 def owner_kernel(cap, rows_in, inc_ref, state_hbm, emb_hbm, nemb_hbm, nstate_hbm, ret_ref,
-                 t0, t1, t2, t3, gf, idx_v, cols_v, emb, state_ref, nstate, scales, sems, idx_all):
+                 gf, idx_v, cols_v, emb, state_ref, nstate, scales, sems, idx_all, *tabs):
     devices = idx_v.shape[1]
     owned, columns = emb.shape
-    tabs = (t0, t1, t2, t3)
     gf[...] = inc_ref[...].astype(F32)
     m = gf[pl.ds(cap, devices, stride=rows_in), :]
     index = ((m - 1.0) * LANES + pltpu.roll(m, LANES - cap, 1)).astype(I32)
@@ -111,32 +110,33 @@
 
     def clear(c, carry):
         for t in tabs:
-            t[pl.ds(pl.multiple_of(c * 64, 64), 64), :] = jnp.zeros((64, columns), F32)
-        return carry
-    lax.fori_loop(0, owned // 64, clear, 0)
+            t[pl.ds(pl.multiple_of(c * 256, 256), 256), :] = jnp.zeros((256, columns), F32)
+        return carry
+    lax.fori_loop(0, owned // 256, clear, 0)
     copies[0].wait()
 
     def add(c, carry):
-        for n in range(8):
-            d = c * 8 + n
+        for n in range(32):
+            d = c * 32 + n
             rows = gf.at[pl.ds(d * rows_in, rows_in), :]
             for i in range(0, cap, TABLES):
-                at = [pl.ds(idx_s[i + k][d], 1) for k in range(TABLES)]
-                new = [tabs[k][at[k], :] + rows[i + k:i + k + 1, :] for k in range(TABLES)]
-                for k in range(TABLES):
-                    tabs[k][at[k], :] = new[k]
-        return carry
-    lax.fori_loop(0, devices // 8, add, 0)
+                run = [*zip(tabs, range(i, min(i + TABLES, cap)))]
+                at = [pl.ds(idx_s[k][d], 1) for _, k in run]
+                new = [t[here, :] + rows[k:k + 1, :] for (t, k), here in zip(run, at)]
+                for (t, _), here, value in zip(run, at, new):
+                    t[here, :] = value
+        return carry
+    lax.fori_loop(0, devices // 32, add, 0)
     load_state.wait()
 
-    per = 8
+    per = 32
 
     def measure(c, carry):
         means = []
         for k in range(per):
             rows = pl.ds(pl.multiple_of((c * per + k) * LANES, LANES), LANES)
-            total = (t0[rows, :] + t1[rows, :]) + (t2[rows, :] + t3[rows, :])
-            t0[rows, :] = total
+            total = functools.reduce(jnp.add, [t[rows, :] for t in tabs])
+            tabs[0][rows, :] = total
             square = total * total
             high = square.astype(BF16)
             low = (square - high.astype(F32)).astype(BF16)
@@ -157,24 +157,24 @@
 
     cols_v[:, 0:owned // LANES] = jnp.transpose(scales[...])
     def update(c, carry):
-        for k in range(8):
-            rows = pl.ds(pl.multiple_of((c * 8 + k) * LANES, LANES), LANES)
-            emb[rows, :] = emb[rows, :] - t0[rows, :] * pick(cols_v[...], c * 8 + k)
-        rows = pl.ds(pl.multiple_of(c * 8 * LANES, 8 * LANES), 8 * LANES)
+        for k in range(16):
+            rows = pl.ds(pl.multiple_of((c * 16 + k) * LANES, LANES), LANES)
+            emb[rows, :] = emb[rows, :] - tabs[0][rows, :] * pick(cols_v[...], c * 16 + k)
+        rows = pl.ds(pl.multiple_of(c * 16 * LANES, 16 * LANES), 16 * LANES)
         pltpu.make_async_copy(emb.at[rows, :], nemb_hbm.at[rows, :], sems.at[2]).start()
         return carry
-    lax.fori_loop(0, owned // (8 * LANES), update, 0)
+    lax.fori_loop(0, owned // (16 * LANES), update, 0)
 
     copies[1].wait()
 
     def fetch(c, carry):
-        for n in range(8):
-            d = c * 8 + n
+        for n in range(16):
+            d = c * 16 + n
             rows = gf.at[pl.ds(pl.multiple_of(d * cap, cap), cap), :]
             for i in range(cap):
                 rows[i:i + 1, :] = emb[pl.ds(idx_s[cap + i][d], 1), :]
         return carry
-    lax.fori_loop(0, devices // 8, fetch, 0)
+    lax.fori_loop(0, devices // 16, fetch, 0)
     ret_ref[...] = gf[0:devices * cap, :].astype(BF16)
     out_state.wait()
     pltpu.make_async_copy(emb, nemb_hbm, sems.at[2]).wait()
@@ -244,8 +244,7 @@
         ),
         in_specs=[VM, ANY, ANY],
         out_specs=(ANY, ANY, VM),
-        scratch_shapes=[pltpu.VMEM((owned, columns), F32)] * TABLES
-        + [
+        scratch_shapes=[
             pltpu.VMEM((devices * rows_out, columns), F32),
             pltpu.VMEM((LANES, devices), I32),
             pltpu.VMEM((LANES, LANES), F32),
@@ -255,7 +254,7 @@
             pltpu.VMEM((owned // LANES, LANES), F32),
             pltpu.SemaphoreType.DMA((6,)),
             pltpu.SMEM((2 * cap, devices), I32),
-        ],
+        ] + [pltpu.VMEM((owned, columns), F32)] * TABLES,
         compiler_params=pltpu.CompilerParams(vmem_limit_bytes=36 << 20),
         name="owner",
     )(incoming, in_hbm(adagrad_state.reshape(owned // LANES, LANES)), in_hbm(embedding))

time: 72.2 us -> 70.8 us (0.981)
  Pallas kernels: 17.4 us -> 16 us
    pallas_call x1, Pallas kernels: 12.8 us -> 11.4 us  [on_device(): pl.pallas_call(functools.partial(owner_kernel, cap, rows_out), out_shape=...]
where the time goes in v7:
time: 70.8 us; the launch traced here: 70.7 us
  blocking collectives  54 us (76%)
  Pallas kernels  16 us (23%)
    all_to_all x1, blocking collectives, exchange(): x = lax.all_to_all(x, AXES, split_axis=0, concat_axis=0, tiled=True)  30.8 us
    all_to_all x1, blocking collectives, on_device(): lax.all_to_all(fetched.reshape(devices, cap, columns), AXES, split_axis=0...  23.3 us
    pallas_call x1, Pallas kernels, on_device(): pl.pallas_call(functools.partial(owner_kernel, cap, rows_out), out_shape=...  11.4 us
    pallas_call x1, Pallas kernels, on_device(): pl.pallas_call(functools.partial(pack_kernel, cap, rows_out), out_shape=(...  2.67 us
    pallas_call x1, Pallas kernels, on_device(): pl.pallas_call(unpack_kernel, out_shape=shape((lookups, columns), BF16),...  1.96 us

profile of v7, /device:TPU:1, one launch (start us, length us, event | category | flops | bytes accessed | tf_op | source)
XLA Modules:
  0.0 70.7 jit_solution(14500472734859845253)
XLA Ops:
  0.6 2.7 %pack.1 = (bf16[4352,128]{1,0:T(8,128)(2,1)S(1)}, s32[8,128]{1,0:T(8,128)S(1)}) custom-call(s32[8,128]{1,0:T(8,128)} %bitcast.15, s32[8,128]{1,0:T(8,128)} %bitcast.16, s32[8,128]{1,0:T(8,128)} %bitcast.17, s32[8,128]{1,0:T(8,128)} %bitcast.18, bf16[1024,128]{1,0:T(8,128)(2,1)} %g_hbm.1), custom_call_target="tpu_custom_call" | custom-call | tf_op jit(solution)/shard_map/pack/pallas_call | solution.py:213
  3.3 30.8 %all_to_all.10 = bf16[128,17,2,128]{3,2,1,0:T(2,128)(2,1)S(1)} all-to-all(bf16[128,17,2,128]{3,2,1,0:T(2,128)(2,1)S(1)} %bitcast.12), channel_id=1, replica_groups=mesh['dp'=4,'rows'=32] {'dp','rows'}, dimensions={0} | all-to-all | bytes 2228224 | tf_op jit(solution)/shard_map/all_to_all | solution.py:233
  34.1 11.4 %owner.1 = (f32[8192,128]{1,0:T(8,128)}, f32[64,128]{1,0:T(8,128)}, bf16[4096,128]{1,0:T(8,128)(2,1)S(1)}) custom-call(bf16[4352,128]{1,0:T(8,128)(2,1)S(1)} %bitcast.10, f32[64,128]{1,0:T(8,128)} %bitcast.14, f32[8192,128]{1,0:T(8,128)} %emb_hbm.1), custom_call_target="tpu_custom_call" | custom-call | tf_op jit(solution)/shard_map/owner/pallas_call | solution.py:238
  45.5 23.3 %all_to_all.11 = bf16[128,32,128]{2,1,0:T(8,128)(2,1)S(1)} all-to-all(bf16[128,32,128]{2,1,0:T(8,128)(2,1)S(1)} %bitcast.13), channel_id=1, replica_groups=mesh['dp'=4,'rows'=32] {'dp','rows'}, dimensions={0} | all-to-all | bytes 2097152 | tf_op jit(solution)/shard_map/all_to_all | solution.py:262
  68.7 2.0 %unpack.1 = bf16[1024,128]{1,0:T(8,128)(2,1)} custom-call(s32[8,128]{1,0:T(8,128)S(1)} %get-tuple-element.11.q_any, bf16[4096,128]{1,0:T(8,128)(2,1)S(1)} %bitcast.11), custom_call_target="tpu_custom_call" | custom-call | tf_op jit(solution)/shard_map/unpack/pallas_call | solution.py:266

commit v8 on v7

--- a/solution.py
+++ b/solution.py
@@ -75,11 +75,11 @@
     copy.wait()
 
     def place(i, carry):
-        for u in range(16):
+        for u in range(32):
             for b in range(blocks):
-                outf[pl.ds(pos_s.at[b][i * 16 + u], 1), :] = gf[pl.ds(b * LANES + i * 16 + u, 1), :]
-        return carry
-    lax.fori_loop(0, LANES // 16, place, 0)
+                outf[pl.ds(pos_s.at[b][i * 32 + u], 1), :] = gf[pl.ds(b * LANES + i * 32 + u, 1), :]
+        return carry
+    lax.fori_loop(0, LANES // 32, place, 0)
     out_ref[...] = outf[...].astype(BF16)
 
 
@@ -129,6 +129,7 @@
     lax.fori_loop(0, devices // 32, add, 0)
     load_state.wait()
 
+    eye = iota((LANES, LANES), 0) == iota((LANES, LANES), 1)
     per = 32
 
     def measure(c, carry):
@@ -138,13 +139,17 @@
             total = functools.reduce(jnp.add, [t[rows, :] for t in tabs])
             tabs[0][rows, :] = total
             square = total * total
-            high = square.astype(BF16)
-            low = (square - high.astype(F32)).astype(BF16)
-            both = lax.dot_general(
-                jnp.ones((8, 2 * columns), BF16), jnp.concatenate([high, low], axis=1),
-                (((1,), (1,)), ((), ())), preferred_element_type=F32,
-            )
-            means.append(both[0:1, :])
+            if k % 2:
+                mean = jnp.sum(square, axis=1, keepdims=True)
+                means.append(jnp.sum(jnp.where(eye, mean, 0.0), axis=0, keepdims=True))
+            else:
+                high = square.astype(BF16)
+                low = (square - high.astype(F32)).astype(BF16)
+                both = lax.dot_general(
+                    jnp.ones((8, 2 * columns), BF16), jnp.concatenate([high, low], axis=1),
+                    (((1,), (1,)), ((), ())), preferred_element_type=F32,
+                )
+                means.append(both[0:1, :])
         here = pl.ds(pl.multiple_of(c * per, per), per)
         state = state_ref[here, :] + jnp.concatenate(means, axis=0) * (1.0 / columns)
         nstate[here, :] = state
@@ -157,13 +162,13 @@
 
     cols_v[:, 0:owned // LANES] = jnp.transpose(scales[...])
     def update(c, carry):
-        for k in range(16):
-            rows = pl.ds(pl.multiple_of((c * 16 + k) * LANES, LANES), LANES)
-            emb[rows, :] = emb[rows, :] - tabs[0][rows, :] * pick(cols_v[...], c * 16 + k)
-        rows = pl.ds(pl.multiple_of(c * 16 * LANES, 16 * LANES), 16 * LANES)
+        for k in range(32):
+            rows = pl.ds(pl.multiple_of((c * 32 + k) * LANES, LANES), LANES)
+            emb[rows, :] = emb[rows, :] - tabs[0][rows, :] * pick(cols_v[...], c * 32 + k)
+        rows = pl.ds(pl.multiple_of(c * 32 * LANES, 32 * LANES), 32 * LANES)
         pltpu.make_async_copy(emb.at[rows, :], nemb_hbm.at[rows, :], sems.at[2]).start()
         return carry
-    lax.fori_loop(0, owned // (16 * LANES), update, 0)
+    lax.fori_loop(0, owned // (32 * LANES), update, 0)
 
     copies[1].wait()
 
@@ -187,11 +192,11 @@
     copy.wait()
 
     def take(i, carry):
-        for u in range(16):
+        for u in range(32):
             for b in range(q_ref.shape[0]):
-                rows[pl.ds(b * LANES + i * 16 + u, 1), :] = wide[pl.ds(q_ref.at[b][i * 16 + u], 1), :]
-        return carry
-    lax.fori_loop(0, LANES // 16, take, 0)
+                rows[pl.ds(b * LANES + i * 32 + u, 1), :] = wide[pl.ds(q_ref.at[b][i * 32 + u], 1), :]
+        return carry
+    lax.fori_loop(0, LANES // 32, take, 0)
     out_ref[...] = rows[...].astype(BF16)
 
 

time: 70.8 us -> 70.5 us (level)
  no operation moved by 1% of the time
where the time goes in v8:
time: 70.5 us; the launch traced here: 70.3 us
  blocking collectives  54 us (77%)
  Pallas kernels  15.7 us (22%)
    all_to_all x1, blocking collectives, exchange(): x = lax.all_to_all(x, AXES, split_axis=0, concat_axis=0, tiled=True)  30.8 us
    all_to_all x1, blocking collectives, on_device(): lax.all_to_all(fetched.reshape(devices, cap, columns), AXES, split_axis=0...  23.3 us
    pallas_call x1, Pallas kernels, on_device(): pl.pallas_call(functools.partial(owner_kernel, cap, rows_out), out_shape=...  11.1 us
    pallas_call x1, Pallas kernels, on_device(): pl.pallas_call(functools.partial(pack_kernel, cap, rows_out), out_shape=(...  2.61 us
    pallas_call x1, Pallas kernels, on_device(): pl.pallas_call(unpack_kernel, out_shape=shape((lookups, columns), BF16),...  1.93 us

profile of v8, /device:TPU:1, one launch (start us, length us, event | category | flops | bytes accessed | tf_op | source)
XLA Modules:
  0.0 70.3 jit_solution(16677331534020316969)
XLA Ops:
  0.6 2.6 %pack.1 = (bf16[4352,128]{1,0:T(8,128)(2,1)S(1)}, s32[8,128]{1,0:T(8,128)S(1)}) custom-call(s32[8,128]{1,0:T(8,128)} %bitcast.15, s32[8,128]{1,0:T(8,128)} %bitcast.16, s32[8,128]{1,0:T(8,128)} %bitcast.17, s32[8,128]{1,0:T(8,128)} %bitcast.18, bf16[1024,128]{1,0:T(8,128)(2,1)} %g_hbm.1), custom_call_target="tpu_custom_call" | custom-call | tf_op jit(solution)/shard_map/pack/pallas_call | solution.py:218
  3.3 30.8 %all_to_all.10 = bf16[128,17,2,128]{3,2,1,0:T(2,128)(2,1)S(1)} all-to-all(bf16[128,17,2,128]{3,2,1,0:T(2,128)(2,1)S(1)} %bitcast.12), channel_id=1, replica_groups=mesh['dp'=4,'rows'=32] {'dp','rows'}, dimensions={0} | all-to-all | bytes 2228224 | tf_op jit(solution)/shard_map/all_to_all | solution.py:238
  34.0 11.1 %owner.1 = (f32[8192,128]{1,0:T(8,128)}, f32[64,128]{1,0:T(8,128)}, bf16[4096,128]{1,0:T(8,128)(2,1)S(1)}) custom-call(bf16[4352,128]{1,0:T(8,128)(2,1)S(1)} %bitcast.10, f32[64,128]{1,0:T(8,128)} %bitcast.14, f32[8192,128]{1,0:T(8,128)} %emb_hbm.1), custom_call_target="tpu_custom_call" | custom-call | tf_op jit(solution)/shard_map/owner/pallas_call | solution.py:243
  45.2 23.3 %all_to_all.11 = bf16[128,32,128]{2,1,0:T(8,128)(2,1)S(1)} all-to-all(bf16[128,32,128]{2,1,0:T(8,128)(2,1)S(1)} %bitcast.13), channel_id=1, replica_groups=mesh['dp'=4,'rows'=32] {'dp','rows'}, dimensions={0} | all-to-all | bytes 2097152 | tf_op jit(solution)/shard_map/all_to_all | solution.py:267
  68.4 1.9 %unpack.1 = bf16[1024,128]{1,0:T(8,128)(2,1)} custom-call(s32[8,128]{1,0:T(8,128)S(1)} %get-tuple-element.11.q_any, bf16[4096,128]{1,0:T(8,128)(2,1)S(1)} %bitcast.11), custom_call_target="tpu_custom_call" | custom-call | tf_op jit(solution)/shard_map/unpack/pallas_call | solution.py:271

commit v9 on v7

--- a/solution.py
+++ b/solution.py
@@ -18,7 +18,7 @@
 
 
 def pack_kernel(cap, rows_out, own_hbm, off_hbm, nown_hbm, noff_hbm, g_hbm, out_ref, q_ref,
-                own_ref, off_ref, nown_ref, noff_ref, g_ref, gf, outf, pos_v, pos_s, sems):
+                t0, t1, own_ref, off_ref, nown_ref, noff_ref, g_ref, gf, outf, pos_v, pos_s, sems):
     loads = [
         pltpu.make_async_copy(src, dst, sems.at[k])
         for k, (src, dst) in enumerate((
@@ -28,6 +28,12 @@
     for load in loads:
         load.start()
     outf[...] = jnp.zeros_like(outf)
+
+    def clear(c, carry):
+        for t in (t0, t1):
+            t[pl.ds(pl.multiple_of(c * 256, 256), 256), :] = jnp.zeros((256, t.shape[1]), F32)
+        return carry
+    lax.fori_loop(0, t0.shape[0] // 256, clear, 0)
     blocks = own_ref.shape[0]
     devices = out_ref.shape[0] // rows_out
     counts = jnp.concatenate(
@@ -87,10 +93,11 @@
     return jnp.take_along_axis(x, jnp.full(x.shape, lane, I32), axis=1)
 
 
-def owner_kernel(cap, rows_in, inc_ref, state_hbm, emb_hbm, nemb_hbm, nstate_hbm, ret_ref,
-                 gf, idx_v, cols_v, emb, state_ref, nstate, scales, sems, idx_all, *tabs):
+def owner_kernel(cap, rows_in, inc_ref, state_hbm, emb_hbm, _0, _1, nemb_hbm, nstate_hbm, ret_ref,
+                 t0, t1, gf, idx_v, cols_v, emb, state_ref, nstate, scales, sems, idx_all, *more):
     devices = idx_v.shape[1]
     owned, columns = emb.shape
+    tabs = (t0, t1, *more)
     gf[...] = inc_ref[...].astype(F32)
     m = gf[pl.ds(cap, devices, stride=rows_in), :]
     index = ((m - 1.0) * LANES + pltpu.roll(m, LANES - cap, 1)).astype(I32)
@@ -109,7 +116,7 @@
     load_state.start()
 
     def clear(c, carry):
-        for t in tabs:
+        for t in more:
             t[pl.ds(pl.multiple_of(c * 256, 256), 256), :] = jnp.zeros((256, columns), F32)
         return carry
     lax.fori_loop(0, owned // 256, clear, 0)
@@ -210,11 +217,12 @@
     view = lambda x: x.reshape(blocks, LANES)
     in_hbm = lambda x: pltpu.with_memory_space_constraint(x, pltpu.HBM)
 
-    outgoing, q = pl.pallas_call(
+    table = pltpu.VMEM((owned, columns), F32)
+    outgoing, q, *tables = pl.pallas_call(
         functools.partial(pack_kernel, cap, rows_out),
-        out_shape=(shape((devices * rows_out, columns), BF16), shape((blocks, LANES), I32)),
+        out_shape=(shape((devices * rows_out, columns), BF16), shape((blocks, LANES), I32), table, table),
         in_specs=[ANY] * 5,
-        out_specs=(VM, VM),
+        out_specs=(VM,) * 4,
         scratch_shapes=[pltpu.VMEM((blocks, LANES), I32)] * 4
         + [
             pltpu.VMEM((lookups, columns), BF16),
@@ -241,9 +249,11 @@
             shape(embedding.shape, F32),
             shape((owned // LANES, LANES), F32),
             shape((devices * cap, columns), BF16),
+            table,
+            table,
         ),
-        in_specs=[VM, ANY, ANY],
-        out_specs=(ANY, ANY, VM),
+        in_specs=[VM, ANY, ANY, VM, VM],
+        out_specs=(ANY, ANY, VM, VM, VM),
         scratch_shapes=[
             pltpu.VMEM((devices * rows_out, columns), F32),
             pltpu.VMEM((LANES, devices), I32),
@@ -254,10 +264,12 @@
             pltpu.VMEM((owned // LANES, LANES), F32),
             pltpu.SemaphoreType.DMA((6,)),
             pltpu.SMEM((2 * cap, devices), I32),
-        ] + [pltpu.VMEM((owned, columns), F32)] * TABLES,
-        compiler_params=pltpu.CompilerParams(vmem_limit_bytes=36 << 20),
+        ] + [pltpu.VMEM((owned, columns), F32)] * (TABLES - 2),
+        input_output_aliases={3: 3, 4: 4},
+        compiler_params=pltpu.CompilerParams(vmem_limit_bytes=24 << 20),
         name="owner",
-    )(incoming, in_hbm(adagrad_state.reshape(owned // LANES, LANES)), in_hbm(embedding))
+    )(incoming, in_hbm(adagrad_state.reshape(owned // LANES, LANES)), in_hbm(embedding),
+      *[pltpu.with_memory_space_constraint(t, pltpu.VMEM) for t in tables])[:3]
 
     returned = lax.all_to_all(
         fetched.reshape(devices, cap, columns), AXES, split_axis=0, concat_axis=0, tiled=True

time: 70.8 us -> 71.4 us (level)
  no operation moved by 1% of the time
where the time goes in v9:
time: 71.4 us; the launch traced here: 71.3 us
  blocking collectives  54 us (76%)
  Pallas kernels  16.6 us (23%)
    all_to_all x1, blocking collectives, exchange(): x = lax.all_to_all(x, AXES, split_axis=0, concat_axis=0, tiled=True)  30.8 us
    all_to_all x1, blocking collectives, on_device(): lax.all_to_all(fetched.reshape(devices, cap, columns), AXES, split_axis=0...  23.3 us
    pallas_call x1, Pallas kernels, on_device(): pl.pallas_call(functools.partial(owner_kernel, cap, rows_out), out_shape=...  11.9 us
    pallas_call x1, Pallas kernels, on_device(): pl.pallas_call(functools.partial(pack_kernel, cap, rows_out), out_shape=(...  2.69 us
    pallas_call x1, Pallas kernels, on_device(): pl.pallas_call(unpack_kernel, out_shape=shape((lookups, columns), BF16),...  1.96 us

profile of v9, /device:TPU:1, one launch (start us, length us, event | category | flops | bytes accessed | tf_op | source)
XLA Modules:
  0.0 71.3 jit_solution(14651700846161767437)
XLA Ops:
  0.6 2.7 %pack.1 = (bf16[4352,128]{1,0:T(8,128)(2,1)S(1)}, s32[8,128]{1,0:T(8,128)S(1)}, f32[8192,128]{1,0:T(8,128)S(1)}, f32[8192,128]{1,0:T(8,128)S(1)}) custom-call(s32[8,128]{1,0:T(8,128)} %bitcast.15, s32[8,128]{1,0:T(8,128)} %bitcast.16, s32[8,128]{1,0:T(8,128)} %bitcast.17, s32[8,128]{1,0:T(8,128)} %bitcast.18, bf16[1024,128]{1,0:T(8,128)(2,1)} %g_hbm.1), custom_call_target="tpu_custom_call" | custom-call | tf_op jit(solution)/shard_map/pack/pallas_call | solution.py:221
  3.3 30.8 %all_to_all.10 = bf16[128,17,2,128]{3,2,1,0:T(2,128)(2,1)S(1)} all-to-all(bf16[128,17,2,128]{3,2,1,0:T(2,128)(2,1)S(1)} %bitcast.12), channel_id=1, replica_groups=mesh['dp'=4,'rows'=32] {'dp','rows'}, dimensions={0} | all-to-all | bytes 2228224 | tf_op jit(solution)/shard_map/all_to_all | solution.py:241
  34.1 11.9 %owner.1 = (f32[8192,128]{1,0:T(8,128)}, f32[64,128]{1,0:T(8,128)}, bf16[4096,128]{1,0:T(8,128)(2,1)S(1)}, f32[8192,128]{1,0:T(8,128)S(1)}, f32[8192,128]{1,0:T(8,128)S(1)}) custom-call(bf16[4352,128]{1,0:T(8,128)(2,1)S(1)} %bitcast.10, f32[64,128]{1,0:T(8,128)} %bitcast.14, f32[8192,128]{1,0:T(8,128)} %emb_hbm.1, ...), custom_call_target="tpu_custom_call", output_to_operand_aliasing={{3}: (3, {}), {4}: (4, {})} | custom-call | tf_op jit(solution)/shard_map/owner/pallas_call | solution.py:246
  46.0 23.3 %all_to_all.11 = bf16[128,32,128]{2,1,0:T(8,128)(2,1)S(1)} all-to-all(bf16[128,32,128]{2,1,0:T(8,128)(2,1)S(1)} %bitcast.13), channel_id=1, replica_groups=mesh['dp'=4,'rows'=32] {'dp','rows'}, dimensions={0} | all-to-all | bytes 2097152 | tf_op jit(solution)/shard_map/all_to_all | solution.py:274
  69.3 2.0 %unpack.1 = bf16[1024,128]{1,0:T(8,128)(2,1)} custom-call(s32[8,128]{1,0:T(8,128)S(1)} %get-tuple-element.15.q_any, bf16[4096,128]{1,0:T(8,128)(2,1)S(1)} %bitcast.11), custom_call_target="tpu_custom_call" | custom-call | tf_op jit(solution)/shard_map/unpack/pallas_call | solution.py:278

commit v10 on v7

--- a/solution.py
+++ b/solution.py
@@ -157,13 +157,13 @@
 
     cols_v[:, 0:owned // LANES] = jnp.transpose(scales[...])
     def update(c, carry):
-        for k in range(16):
-            rows = pl.ds(pl.multiple_of((c * 16 + k) * LANES, LANES), LANES)
-            emb[rows, :] = emb[rows, :] - tabs[0][rows, :] * pick(cols_v[...], c * 16 + k)
-        rows = pl.ds(pl.multiple_of(c * 16 * LANES, 16 * LANES), 16 * LANES)
+        for k in range(32):
+            rows = pl.ds(pl.multiple_of((c * 32 + k) * LANES, LANES), LANES)
+            emb[rows, :] = emb[rows, :] - tabs[0][rows, :] * pick(cols_v[...], c * 32 + k)
+        rows = pl.ds(pl.multiple_of(c * 32 * LANES, 32 * LANES), 32 * LANES)
         pltpu.make_async_copy(emb.at[rows, :], nemb_hbm.at[rows, :], sems.at[2]).start()
         return carry
-    lax.fori_loop(0, owned // (16 * LANES), update, 0)
+    lax.fori_loop(0, owned // (32 * LANES), update, 0)
 
     copies[1].wait()
 

time: 70.8 us -> 70.7 us (level)
  no operation moved by 1% of the time
where the time goes in v10:
time: 70.7 us; the launch traced here: 70.5 us
  blocking collectives  54 us (76%)
  Pallas kernels  15.9 us (22%)
    all_to_all x1, blocking collectives, exchange(): x = lax.all_to_all(x, AXES, split_axis=0, concat_axis=0, tiled=True)  30.8 us
    all_to_all x1, blocking collectives, on_device(): lax.all_to_all(fetched.reshape(devices, cap, columns), AXES, split_axis=0...  23.3 us
    pallas_call x1, Pallas kernels, on_device(): pl.pallas_call(functools.partial(owner_kernel, cap, rows_out), out_shape=...  11.2 us
    pallas_call x1, Pallas kernels, on_device(): pl.pallas_call(functools.partial(pack_kernel, cap, rows_out), out_shape=(...  2.67 us
    pallas_call x1, Pallas kernels, on_device(): pl.pallas_call(unpack_kernel, out_shape=shape((lookups, columns), BF16),...  1.96 us

profile of v10, /device:TPU:1, one launch (start us, length us, event | category | flops | bytes accessed | tf_op | source)
XLA Modules:
  0.0 70.5 jit_solution(6221616521685347985)
XLA Ops:
  0.6 2.7 %pack.1 = (bf16[4352,128]{1,0:T(8,128)(2,1)S(1)}, s32[8,128]{1,0:T(8,128)S(1)}) custom-call(s32[8,128]{1,0:T(8,128)} %bitcast.15, s32[8,128]{1,0:T(8,128)} %bitcast.16, s32[8,128]{1,0:T(8,128)} %bitcast.17, s32[8,128]{1,0:T(8,128)} %bitcast.18, bf16[1024,128]{1,0:T(8,128)(2,1)} %g_hbm.1), custom_call_target="tpu_custom_call" | custom-call | tf_op jit(solution)/shard_map/pack/pallas_call | solution.py:213
  3.3 30.8 %all_to_all.10 = bf16[128,17,2,128]{3,2,1,0:T(2,128)(2,1)S(1)} all-to-all(bf16[128,17,2,128]{3,2,1,0:T(2,128)(2,1)S(1)} %bitcast.12), channel_id=1, replica_groups=mesh['dp'=4,'rows'=32] {'dp','rows'}, dimensions={0} | all-to-all | bytes 2228224 | tf_op jit(solution)/shard_map/all_to_all | solution.py:233
  34.1 11.2 %owner.1 = (f32[8192,128]{1,0:T(8,128)}, f32[64,128]{1,0:T(8,128)}, bf16[4096,128]{1,0:T(8,128)(2,1)S(1)}) custom-call(bf16[4352,128]{1,0:T(8,128)(2,1)S(1)} %bitcast.10, f32[64,128]{1,0:T(8,128)} %bitcast.14, f32[8192,128]{1,0:T(8,128)} %emb_hbm.1), custom_call_target="tpu_custom_call" | custom-call | tf_op jit(solution)/shard_map/owner/pallas_call | solution.py:238
  45.3 23.3 %all_to_all.11 = bf16[128,32,128]{2,1,0:T(8,128)(2,1)S(1)} all-to-all(bf16[128,32,128]{2,1,0:T(8,128)(2,1)S(1)} %bitcast.13), channel_id=1, replica_groups=mesh['dp'=4,'rows'=32] {'dp','rows'}, dimensions={0} | all-to-all | bytes 2097152 | tf_op jit(solution)/shard_map/all_to_all | solution.py:262
  68.6 2.0 %unpack.1 = bf16[1024,128]{1,0:T(8,128)(2,1)} custom-call(s32[8,128]{1,0:T(8,128)S(1)} %get-tuple-element.11.q_any, bf16[4096,128]{1,0:T(8,128)(2,1)S(1)} %bitcast.11), custom_call_target="tpu_custom_call" | custom-call | tf_op jit(solution)/shard_map/unpack/pallas_call | solution.py:266
